TPU v7x, 32 devices: a whole 2x2x4 slice. The times are simulated.
32 devices in a mesh: clip: 8 (over z, x), row: 4 (over y, core).
Axes of the slice: x: 2, y: 2, z: 4, core: 2. Of those that a mesh axis runs over, the one named last changes fastest.
Arguments:
- features: bfloat16 [8, 128, 32, 256], P('clip', None, 'row'), may hold values from -6 to 6
- out_weight: bfloat16 [3, 128, 3, 3], replicated, may hold values from -0.1875 to 0.1875
- out_bias: float32 [3], replicated, may hold values from -0.5 to 0.5
- targets: bfloat16 [8, 3, 32, 256], P('clip', None, 'row'), may hold values from -1 to 1
- weight_one: bfloat16 [64, 3, 3, 3], replicated, may hold values from -1.25 to 1.25
- bias_one: float32 [64], replicated, may hold values from -0.2 to 0.2
- weight_two: bfloat16 [64, 64, 3, 3], replicated, may hold values from -0.375 to 0.375
- bias_two: float32 [64], replicated, may hold values from -0.2 to 0.2
- weight_three: bfloat16 [128, 64, 3, 3], replicated, may hold values from -0.375 to 0.375
- bias_three: float32 [128], replicated, may hold values from -0.2 to 0.2
- weight_four: bfloat16 [128, 128, 3, 3], replicated, may hold values from -0.25 to 0.25
- bias_four: float32 [128], replicated, may hold values from -0.2 to 0.2
- lin_one: float32 [64], replicated, may hold values from 0.05 to 0.5
- lin_two: float32 [128], replicated, may hold values from 0.05 to 0.5
Outputs:
- loss: float32 [], replicated
- feature_grad: bfloat16 [8, 128, 32, 256], P('clip', None, 'row')
- out_weight_grad: float32 [3, 128, 3, 3], replicated
- out_bias_grad: float32 [3], replicated
All inputs are finite; a program needn't handle non-finite values.
Results may differ from a plain program's by a relative error of at most 0.02.
Values may be sent and summed in bfloat16 or wider, within the bound.
No kernel may reach another device: no remote copies, remote signals or barrier semaphores. Data moves between devices by JAX's collectives and lax.ppermute only.
A program may use at most 64 MiB of HBM per device.

v0:
```python
import math

import jax
import jax.numpy as jnp
from jax import lax
from jax.sharding import PartitionSpec as P

shift_values = [-0.03, -0.088, -0.188]
scale_values = [0.458, 0.448, 0.45]


def padded_2(array, sides, width):
    for axis, dim in sides:
        size, length = (lax.axis_size(axis), array.shape[dim])
        up = [(i, (i + 1) % size) for i in range(size - 1)]
        down = [(j, i) for i, j in up]
        last = lax.slice_in_dim(array, length - width, length, axis=dim)
        leading = lax.slice_in_dim(array, 0, width, axis=dim)
        before = lax.ppermute(last, axis, up)
        after = lax.ppermute(leading, axis, down)
        array = jnp.concatenate([before, array, after], axis=dim)
    return array


def shifted(array, axis, by):
    size = lax.axis_size(axis)
    pairs = [(i, i + by) for i in range(size) if 0 <= i + by < size]
    return lax.ppermute(array, axis, pairs)


def shift_array():
    return jnp.array(shift_values, jnp.float32).reshape(1, 3, 1, 1)


def scale_array():
    return jnp.array(scale_values, jnp.float32).reshape(1, 3, 1, 1)


def gelu_exact(values):
    return values * 0.5 * (1.0 + jax.scipy.special.erf(values / math.sqrt(2.0)))


def gelu_slope(values):
    normal_cdf = 0.5 * (1.0 + jax.scipy.special.erf(values / math.sqrt(2.0)))
    density = jnp.exp(-0.5 * values * values) / math.sqrt(2.0 * math.pi)
    return normal_cdf + values * density


def pad_rows(inputs):
    return jnp.pad(inputs, ((0, 0), (0, 0), (1, 1), (0, 0)))


def flipped(weight):
    return jnp.flip(weight, (2, 3)).transpose(1, 0, 2, 3)


def conv_valid(padded, weight):
    frame_count, channels, row_total, col_count = padded.shape
    row_count = row_total - 2
    outputs = weight.shape[0]
    wide = jnp.pad(padded, ((0, 0), (0, 0), (0, 0), (1, 1)))
    total = jnp.zeros((outputs, row_count * col_count), jnp.float32)
    for row_shift in range(3):
        for col_shift in range(3):
            piece = wide[0, :, row_shift : row_shift + row_count, col_shift : col_shift + col_count]
            total = total + jnp.dot(
                weight[:, :, row_shift, col_shift],
                piece.reshape(channels, row_count * col_count),
                preferred_element_type=jnp.float32,
            )
    results = [total.reshape(outputs, row_count, col_count)]
    return jnp.stack(results)


def grad_from_output(inputs, grad_pad):
    frame_count, channels, row_count, col_count = inputs.shape
    outputs = grad_pad.shape[1]
    wide = jnp.pad(grad_pad, ((0, 0), (0, 0), (0, 0), (1, 1)))
    blocks = []
    for row_shift in range(3):
        for col_shift in range(3):
            left = wide[
                0,
                :,
                2 - row_shift : 2 - row_shift + row_count,
                2 - col_shift : 2 - col_shift + col_count,
            ].reshape(outputs, row_count * col_count)
            right = inputs[0].reshape(channels, row_count * col_count)
            total = lax.dot_general(
                left, right, (((1,), (1,)), ((), ())), preferred_element_type=jnp.float32
            )
            blocks.append(total)
    return jnp.stack(blocks).reshape(3, 3, outputs, channels).transpose(2, 3, 0, 1)


def edge_terms(row_values, kernel_row):
    col_count = row_values.shape[2]
    wide = jnp.pad(row_values, ((0, 0), (0, 0), (1, 1)))
    total = jnp.zeros((row_values.shape[0], kernel_row.shape[0], col_count), jnp.float32)
    for col_shift in range(3):
        total = total + jnp.einsum(
            "oc,fcw->fow",
            kernel_row[:, :, col_shift],
            wide[:, :, col_shift : col_shift + col_count],
            preferred_element_type=jnp.float32,
        )
    return total


def pool_mean(values):
    frame_count, channels, row_count, col_count = values.shape
    return values.reshape(frame_count, channels, row_count // 2, 2, col_count // 2, 2).mean(
        axis=(3, 5)
    )


def upsample(values):
    return jnp.repeat(jnp.repeat(values, 2, 2), 2, 3)


def vgg_forward(image, weights):
    weight_one, bias_one, weight_two, bias_two, weight_three, bias_three, weight_four, bias_four = (
        weights
    )
    image_pad = padded_2(image, (("row", 2),), 1)
    pre_one = conv_valid(image_pad, weight_one) + bias_one[None, :, None, None]
    act_one = gelu_exact(pre_one).astype(jnp.bfloat16)
    act_pad = padded_2(act_one, (("row", 2),), 1)
    pre_two = conv_valid(act_pad, weight_two) + bias_two[None, :, None, None]
    act_two = gelu_exact(pre_two)
    pooled = pool_mean(act_two).astype(jnp.bfloat16)
    pooled_pad = padded_2(pooled, (("row", 2),), 1)
    pre_three = conv_valid(pooled_pad, weight_three) + bias_three[None, :, None, None]
    act_three = gelu_exact(pre_three).astype(jnp.bfloat16)
    three_pad = padded_2(act_three, (("row", 2),), 1)
    pre_four = conv_valid(three_pad, weight_four) + bias_four[None, :, None, None]
    act_four = gelu_exact(pre_four)
    return (pre_one, pre_two, act_two, pre_three, pre_four, act_four)


def lpips_layer(feat_dec, feat_tgt, lin, count):
    norm_dec = jnp.sqrt(jnp.sum(feat_dec * feat_dec, 1, keepdims=True) + 1e-06)
    norm_tgt = jnp.sqrt(jnp.sum(feat_tgt * feat_tgt, 1, keepdims=True) + 1e-06)
    unit_dec = feat_dec / norm_dec
    differ = unit_dec - feat_tgt / norm_tgt
    scaled = lin[None, :, None, None]
    part = jnp.sum(scaled * differ * differ) / count
    grad_unit = 2.0 * scaled * differ / count
    grad_feat = (grad_unit - unit_dec * jnp.sum(grad_unit * unit_dec, 1, keepdims=True)) / norm_dec
    return (part, grad_feat)


def local(
    features,
    out_weight,
    out_bias,
    targets,
    weight_one,
    bias_one,
    weight_two,
    bias_two,
    weight_three,
    bias_three,
    weight_four,
    bias_four,
    lin_one,
    lin_two,
):
    weights = (
        weight_one,
        bias_one,
        weight_two,
        bias_two,
        weight_three,
        bias_three,
        weight_four,
        bias_four,
    )
    row_count = features.shape[2]
    width = features.shape[3]
    height = row_count * lax.axis_size("row")
    pre_out = conv_valid(pad_rows(features), out_weight)
    down_terms = edge_terms(features[:, :, row_count - 1, :], out_weight[:, :, 0, :])
    up_terms = edge_terms(features[:, :, 0, :], out_weight[:, :, 2, :])
    from_above = shifted(down_terms, "row", 1)
    from_below = shifted(up_terms, "row", -1)
    pre_out = pre_out.at[:, :, 0, :].add(from_above)
    pre_out = pre_out.at[:, :, row_count - 1, :].add(from_below)
    decoded = (pre_out + out_bias[None, :, None, None]).astype(jnp.bfloat16)
    image_dec = ((decoded.astype(jnp.float32) - shift_array()) / scale_array()).astype(jnp.bfloat16)
    image_tgt = ((targets.astype(jnp.float32) - shift_array()) / scale_array()).astype(jnp.bfloat16)
    pre_one, pre_two, act_two, pre_three, pre_four, act_four = vgg_forward(image_dec, weights)
    tgt_acts = vgg_forward(image_tgt, weights)
    part_one, grad_two = lpips_layer(act_two, tgt_acts[2], lin_one, float(height * width))
    part_two, grad_four = lpips_layer(
        act_four, tgt_acts[5], lin_two, float(height // 2 * (width // 2))
    )
    grad_pre4 = (grad_four * gelu_slope(pre_four)).astype(jnp.bfloat16)
    grad_act3 = conv_valid(padded_2(grad_pre4, (("row", 2),), 1), flipped(weight_four))
    grad_pre3 = (grad_act3 * gelu_slope(pre_three)).astype(jnp.bfloat16)
    grad_pool = conv_valid(padded_2(grad_pre3, (("row", 2),), 1), flipped(weight_three))
    grad_pre2 = ((grad_two + 0.25 * upsample(grad_pool)) * gelu_slope(pre_two)).astype(jnp.bfloat16)
    grad_act1 = conv_valid(padded_2(grad_pre2, (("row", 2),), 1), flipped(weight_two))
    grad_pre1 = (grad_act1 * gelu_slope(pre_one)).astype(jnp.bfloat16)
    grad_image = conv_valid(padded_2(grad_pre1, (("row", 2),), 1), flipped(weight_one))
    grad_dec = (grad_image / scale_array()).astype(jnp.bfloat16)
    grad_pad = padded_2(grad_dec, (("row", 2),), 1)
    feature_grad = conv_valid(grad_pad, flipped(out_weight)).astype(jnp.bfloat16)
    weight_grad = grad_from_output(features, grad_pad)
    bias_grad = jnp.sum(grad_dec.astype(jnp.float32), (0, 2, 3))
    loss, weight_total, bias_total = lax.psum(
        (part_one + part_two, weight_grad, bias_grad), ("clip", "row")
    )
    return (loss, feature_grad, weight_total, bias_total)


def solution(mesh):
    placed = (
        P("clip", None, "row", None),
        P(),
        P(),
        P("clip", None, "row", None),
        P(),
        P(),
        P(),
        P(),
        P(),
        P(),
        P(),
        P(),
        P(),
        P(),
    )
    return jax.shard_map(
        local,
        mesh=mesh,
        in_specs=placed,
        out_specs=(P(), P("clip", None, "row", None), P(), P()),
        check_vma=False,
    )
```

profile of v0, /device:TPU:0, one launch (start us, length us, event | category | flops | bytes accessed | tf_op | source)
XLA Modules:
  0.0 208.2 jit_solution(6531382458531928736)
XLA Ops:
  1.4 1.4 fusion.406
  3.4 2.4 %collective-permute-start = (f32[1,3,256]{2,1,0:T(4,128)S(1)}, f32[1,3,256]{2,1,0:T(4,128)S(1)}, u32[]{:S(2)}, u32[]{:S(2)}) collective-permute-start(f32[1,3,256]{2,1,0:T(4,128)S(1)} %fusion.18), channel_id=1, source_target_pairs={{0,1},{1,2},{2,3},{4,5},{5,6},{6,7},{8,9},{9,10},{10,11},{12,13},{... | collective-permute-start | bytes 9224 | tf_op jit(solution)/shard_map/ppermute | solution.py:28
  8.3 1.4 pad_slice_fusion
  15.8 5.2 %collective-permute-start.2 = (bf16[1,3,1,256]{3,1,2,0:T(4,128)(2,1)S(1)}, bf16[1,3,1,256]{3,1,2,0:T(4,128)(2,1)S(1)}, u32[]{:S(2)}, u32[]{:S(2)}) collective-permute-start(bf16[1,3,1,256]{3,1,2,0:T(4,128)(2,1)S(1)} %get-tuple-element.202), channel_id=1, source_target_pairs={{0,1},{1,2},{2,3},{4,5},{5,6},{6,7},{8,9},{9,10},{10,11},{12,13},{... | collective-permute-start | bytes 4616 | tf_op jit(solution)/shard_map/ppermute | solution.py:19
  22.2 4.3 %collective-permute-start.6 = (bf16[1,3,1,256]{3,1,2,0:T(4,128)(2,1)S(1)}, bf16[1,3,1,256]{3,1,2,0:T(4,128)(2,1)S(1)}, u32[]{:S(2)}, u32[]{:S(2)}) collective-permute-start(bf16[1,3,1,256]{3,1,2,0:T(4,128)(2,1)S(1)} %get-tuple-element.198), channel_id=1, source_target_pairs={{0,1},{1,2},{2,3},{4,5},{5,6},{6,7},{8,9},{9,10},{10,11},{12,13},{... | collective-permute-start | bytes 4616 | tf_op jit(solution)/shard_map/ppermute | solution.py:19
  26.5 1.3 collective-permute-start.7
  34.3 4.3 %collective-permute-start.8 = (bf16[1,64,1,256]{3,2,1,0:T(2,128)(2,1)S(1)}, bf16[1,64,1,256]{3,2,1,0:T(2,128)(2,1)S(1)}, u32[]{:S(2)}, u32[]{:S(2)}) collective-permute-start(bf16[1,64,1,256]{3,2,1,0:T(2,128)(2,1)S(1)} %get-tuple-element.108), channel_id=1, source_target_pairs={{0,1},{1,2},{2,3},{4,5},{5,6},{6,7},{8,9},{9,10},{10,11},{12,13},{... | collective-permute-start | bytes 98312 | tf_op jit(solution)/shard_map/ppermute | solution.py:19
  40.1 4.2 %collective-permute-start.4 = (bf16[1,64,1,256]{3,2,1,0:T(2,128)(2,1)S(1)}, bf16[1,64,1,256]{3,2,1,0:T(2,128)(2,1)S(1)}, u32[]{:S(2)}, u32[]{:S(2)}) collective-permute-start(bf16[1,64,1,256]{3,2,1,0:T(2,128)(2,1)S(1)} %get-tuple-element.112), channel_id=1, source_target_pairs={{0,1},{1,2},{2,3},{4,5},{5,6},{6,7},{8,9},{9,10},{10,11},{12,13},{... | collective-permute-start | bytes 98312 | tf_op jit(solution)/shard_map/ppermute | solution.py:19
  44.3 1.5 collective-permute-start.5
  46.1 2.5 %collective-permute-done.5 = bf16[1,64,1,256]{3,2,1,0:T(2,128)(2,1)S(1)} collective-permute-done((bf16[1,64,1,256]{3,2,1,0:T(2,128)(2,1)S(1)}, bf16[1,64,1,256]{3,2,1,0:T(2,128)(2,1)S(1)}, u32[]{:S(2)}, u32[]{:S(2)}) %collective-permute-start.5) | collective-permute-done | bytes 32800 | tf_op jit(solution)/shard_map/ppermute | solution.py:20
  57.6 1.4 copy.256
  60.3 2.1 %copy.253 = f32[1,64,4,2,128,2]{4,1,5,3,2,0:T(8,128)} copy(f32[1,64,4,2,128,2]{1,5,4,3,2,0:T(2,128)} %bitcast.1069) | data formatting | bytes 1048576 | tf_op jit(solution)/shard_map/stack;reshape | solution.py:72
  62.5 2.1 multiply_reduce_fusion.2
  66.5 4.8 %collective-permute-start.14 = (bf16[1,64,1,128]{1,3,2,0:T(8,128)(2,1)S(1)}, bf16[1,64,1,128]{1,3,2,0:T(8,128)(2,1)S(1)}, u32[]{:S(2)}, u32[]{:S(2)}) collective-permute-start(bf16[1,64,1,128]{1,3,2,0:T(8,128)(2,1)S(1)} %get-tuple-element.172), channel_id=1, source_target_pairs={{0,1},{1,2},{2,3},{4,5},{5,6},{6,7},{8,9},{9,10},{10,11},{12,13},{... | collective-permute-start | bytes 49160 | tf_op jit(solution)/shard_map/ppermute | solution.py:19
  71.4 1.4 collective-permute-start.15
  72.8 3.0 %collective-permute-start.10 = (bf16[1,64,1,128]{1,3,2,0:T(8,128)(2,1)S(1)}, bf16[1,64,1,128]{1,3,2,0:T(8,128)(2,1)S(1)}, u32[]{:S(2)}, u32[]{:S(2)}) collective-permute-start(bf16[1,64,1,128]{1,3,2,0:T(8,128)(2,1)S(1)} %get-tuple-element.164), channel_id=1, source_target_pairs={{0,1},{1,2},{2,3},{4,5},{5,6},{6,7},{8,9},{9,10},{10,11},{12,13},{... | collective-permute-start | bytes 49160 | tf_op jit(solution)/shard_map/ppermute | solution.py:19
  77.8 2.0 collective-permute-done.11
  83.6 4.5 %collective-permute-start.16 = (bf16[1,128,1,128]{1,3,2,0:T(8,128)(2,1)S(1)}, bf16[1,128,1,128]{1,3,2,0:T(8,128)(2,1)S(1)}, u32[]{:S(2)}, u32[]{:S(2)}) collective-permute-start(bf16[1,128,1,128]{1,3,2,0:T(8,128)(2,1)S(1)} %get-tuple-element.168), channel_id=1, source_target_pairs={{0,1},{1,2},{2,3},{4,5},{5,6},{6,7},{8,9},{9,10},{10,11},{12,13},{... | collective-permute-start | bytes 98312 | tf_op jit(solution)/shard_map/ppermute | solution.py:19
  88.1 1.3 collective-permute-start.17
  89.5 3.0 %collective-permute-start.12 = (bf16[1,128,1,128]{1,3,2,0:T(8,128)(2,1)S(1)}, bf16[1,128,1,128]{1,3,2,0:T(8,128)(2,1)S(1)}, u32[]{:S(2)}, u32[]{:S(2)}) collective-permute-start(bf16[1,128,1,128]{1,3,2,0:T(8,128)(2,1)S(1)} %get-tuple-element.160), channel_id=1, source_target_pairs={{0,1},{1,2},{2,3},{4,5},{5,6},{6,7},{8,9},{9,10},{10,11},{12,13},{... | collective-permute-start | bytes 98312 | tf_op jit(solution)/shard_map/ppermute | solution.py:19
  100.4 4.7 %collective-permute-start.18 = (bf16[1,128,1,128]{1,3,2,0:T(8,128)(2,1)S(1)}, bf16[1,128,1,128]{1,3,2,0:T(8,128)(2,1)S(1)}, u32[]{:S(2)}, u32[]{:S(2)}) collective-permute-start(bf16[1,128,1,128]{1,3,2,0:T(8,128)(2,1)S(1)} %get-tuple-element.156), channel_id=1, source_target_pairs={{0,1},{1,2},{2,3},{4,5},{5,6},{6,7},{8,9},{9,10},{10,11},{12,13},{... | collective-permute-start | bytes 98312 | tf_op jit(solution)/shard_map/ppermute | solution.py:19
  106.4 1.8 collective-permute-done.19
  110.4 4.1 %collective-permute-start.20 = (bf16[1,128,1,128]{1,3,2,0:T(8,128)(2,1)S(1)}, bf16[1,128,1,128]{1,3,2,0:T(8,128)(2,1)S(1)}, u32[]{:S(2)}, u32[]{:S(2)}) collective-permute-start(bf16[1,128,1,128]{1,3,2,0:T(8,128)(2,1)S(1)} %get-tuple-element.152), channel_id=1, source_target_pairs={{0,1},{1,2},{2,3},{4,5},{5,6},{6,7},{8,9},{9,10},{10,11},{12,13},{... | collective-permute-start | bytes 98312 | tf_op jit(solution)/shard_map/ppermute | solution.py:19
  114.5 1.5 collective-permute-start.21
  116.1 1.7 multiply_reduce_fusion
  124.0 2.0 fusion.35
  126.7 3.6 %collective-permute-start.22 = (bf16[1,64,1,256]{3,2,1,0:T(2,128)(2,1)}, bf16[1,64,1,256]{3,2,1,0:T(2,128)(2,1)}, u32[]{:S(2)}, u32[]{:S(2)}) collective-permute-start(bf16[1,64,1,256]{3,2,1,0:T(2,128)(2,1)} %get-tuple-element.104), channel_id=1, source_target_pairs={{0,1},{1,2},{2,3},{4,5},{5,6},{6,7},{8,9},{9,10},{10,11},{12,13},{... | collective-permute-start | bytes 98312 | tf_op jit(solution)/shard_map/ppermute | solution.py:19
  141.2 3.3 %collective-permute-start.24 = (bf16[1,64,1,256]{3,2,1,0:T(2,128)(2,1)S(1)}, bf16[1,64,1,256]{3,2,1,0:T(2,128)(2,1)S(1)}, u32[]{:S(2)}, u32[]{:S(2)}) collective-permute-start(bf16[1,64,1,256]{3,2,1,0:T(2,128)(2,1)S(1)} %get-tuple-element.100), channel_id=1, source_target_pairs={{0,1},{1,2},{2,3},{4,5},{5,6},{6,7},{8,9},{9,10},{10,11},{12,13},{... | collective-permute-start | bytes 98312 | tf_op jit(solution)/shard_map/ppermute | solution.py:19
  146.0 2.8 %collective-permute-done.25 = bf16[1,64,1,256]{3,2,1,0:T(2,128)(2,1)S(1)} collective-permute-done((bf16[1,64,1,256]{3,2,1,0:T(2,128)(2,1)S(1)}, bf16[1,64,1,256]{3,2,1,0:T(2,128)(2,1)S(1)}, u32[]{:S(2)}, u32[]{:S(2)}) %collective-permute-start.25) | collective-permute-done | bytes 32800 | tf_op jit(solution)/shard_map/ppermute | solution.py:20
  151.5 4.8 %collective-permute-start.26 = (bf16[1,3,1,256]{3,1,2,0:T(4,128)(2,1)S(1)}, bf16[1,3,1,256]{3,1,2,0:T(4,128)(2,1)S(1)}, u32[]{:S(2)}, u32[]{:S(2)}) collective-permute-start(bf16[1,3,1,256]{3,1,2,0:T(4,128)(2,1)S(1)} %get-tuple-element.194), channel_id=1, source_target_pairs={{0,1},{1,2},{2,3},{4,5},{5,6},{6,7},{8,9},{9,10},{10,11},{12,13},{... | collective-permute-start | bytes 4616 | tf_op jit(solution)/shard_map/ppermute | solution.py:19
  156.4 1.6 collective-permute-start.27
  166.7 41.5 %all-reduce.17 = (f32[]{:T(128)}, f32[3,128,3,3]{1,3,2,0:T(4,128)}, f32[3]{0:T(128)}) all-reduce(f32[]{:T(128)S(6)} %add.1136, f32[3,128,3,3]{1,3,2,0:T(4,128)S(1)} %bitcast.1222, f32[3]{0:T(128)S(1)} %get-tuple-element.57), channel_id=1, replica_groups=mesh['clip'=8,'row'=4] {'clip','row'}, use_global_device_ids=true, to_apply=%region_8.9 | all-reduce | flops 3460 | bytes 27680 | tf_op jit(solution)/shard_map/psum | solution.py:211
  (410 shorter events, 76.5 us)
Async XLA Ops:
  0.6 7.1 %copy-start = (bf16[1,128,8,256]{3,2,1,0:T(8,128)(2,1)S(1)}, bf16[1,128,8,256]{3,2,1,0:T(8,128)(2,1)}, u32[]{:S(2)}) copy-start(bf16[1,128,8,256]{3,2,1,0:T(8,128)(2,1)} %param.23) | copy-start | bytes 1572868
  3.4 12.2 %collective-permute-start = (f32[1,3,256]{2,1,0:T(4,128)S(1)}, f32[1,3,256]{2,1,0:T(4,128)S(1)}, u32[]{:S(2)}, u32[]{:S(2)}) collective-permute-start(f32[1,3,256]{2,1,0:T(4,128)S(1)} %fusion.18), channel_id=1, source_target_pairs={{0,1},{1,2},{2,3},{4,5},{5,6},{6,7},{8,9},{9,10},{10,11},{12,13},{... | collective-permute-start | bytes 9224 | tf_op jit(solution)/shard_map/ppermute | solution.py:28
  6.4 9.2 %collective-permute-start.1 = (f32[1,3,256]{2,1,0:T(4,128)S(1)}, f32[1,3,256]{2,1,0:T(4,128)S(1)}, u32[]{:S(2)}, u32[]{:S(2)}) collective-permute-start(f32[1,3,256]{2,1,0:T(4,128)S(1)} %fusion.17), channel_id=1, source_target_pairs={{1,0},{2,1},{3,2},{5,4},{6,5},{7,6},{9,8},{10,9},{11,10},{13,12},{... | collective-permute-start | bytes 9224 | tf_op jit(solution)/shard_map/ppermute | solution.py:28
  15.8 12.1 %collective-permute-start.2 = (bf16[1,3,1,256]{3,1,2,0:T(4,128)(2,1)S(1)}, bf16[1,3,1,256]{3,1,2,0:T(4,128)(2,1)S(1)}, u32[]{:S(2)}, u32[]{:S(2)}) collective-permute-start(bf16[1,3,1,256]{3,1,2,0:T(4,128)(2,1)S(1)} %get-tuple-element.202), channel_id=1, source_target_pairs={{0,1},{1,2},{2,3},{4,5},{5,6},{6,7},{8,9},{9,10},{10,11},{12,13},{... | collective-permute-start | bytes 4616 | tf_op jit(solution)/shard_map/ppermute | solution.py:19
  20.9 6.9 %collective-permute-start.3 = (bf16[1,3,1,256]{3,1,2,0:T(4,128)(2,1)S(1)}, bf16[1,3,1,256]{3,1,2,0:T(4,128)(2,1)S(1)}, u32[]{:S(2)}, u32[]{:S(2)}) collective-permute-start(bf16[1,3,1,256]{3,1,2,0:T(4,128)(2,1)S(1)} %get-tuple-element.203), channel_id=1, source_target_pairs={{1,0},{2,1},{3,2},{5,4},{6,5},{7,6},{9,8},{10,9},{11,10},{13,12},{... | collective-permute-start | bytes 4616 | tf_op jit(solution)/shard_map/ppermute | solution.py:20
  22.2 8.5 %collective-permute-start.6 = (bf16[1,3,1,256]{3,1,2,0:T(4,128)(2,1)S(1)}, bf16[1,3,1,256]{3,1,2,0:T(4,128)(2,1)S(1)}, u32[]{:S(2)}, u32[]{:S(2)}) collective-permute-start(bf16[1,3,1,256]{3,1,2,0:T(4,128)(2,1)S(1)} %get-tuple-element.198), channel_id=1, source_target_pairs={{0,1},{1,2},{2,3},{4,5},{5,6},{6,7},{8,9},{9,10},{10,11},{12,13},{... | collective-permute-start | bytes 4616 | tf_op jit(solution)/shard_map/ppermute | solution.py:19
  26.5 4.3 %collective-permute-start.7 = (bf16[1,3,1,256]{3,1,2,0:T(4,128)(2,1)S(1)}, bf16[1,3,1,256]{3,1,2,0:T(4,128)(2,1)S(1)}, u32[]{:S(2)}, u32[]{:S(2)}) collective-permute-start(bf16[1,3,1,256]{3,1,2,0:T(4,128)(2,1)S(1)} %get-tuple-element.199), channel_id=1, source_target_pairs={{1,0},{2,1},{3,2},{5,4},{6,5},{7,6},{9,8},{10,9},{11,10},{13,12},{... | collective-permute-start | bytes 4616 | tf_op jit(solution)/shard_map/ppermute | solution.py:20
  34.3 11.5 %collective-permute-start.8 = (bf16[1,64,1,256]{3,2,1,0:T(2,128)(2,1)S(1)}, bf16[1,64,1,256]{3,2,1,0:T(2,128)(2,1)S(1)}, u32[]{:S(2)}, u32[]{:S(2)}) collective-permute-start(bf16[1,64,1,256]{3,2,1,0:T(2,128)(2,1)S(1)} %get-tuple-element.108), channel_id=1, source_target_pairs={{0,1},{1,2},{2,3},{4,5},{5,6},{6,7},{8,9},{9,10},{10,11},{12,13},{... | collective-permute-start | bytes 98312 | tf_op jit(solution)/shard_map/ppermute | solution.py:19
  38.5 7.2 %collective-permute-start.9 = (bf16[1,64,1,256]{3,2,1,0:T(2,128)(2,1)S(1)}, bf16[1,64,1,256]{3,2,1,0:T(2,128)(2,1)S(1)}, u32[]{:S(2)}, u32[]{:S(2)}) collective-permute-start(bf16[1,64,1,256]{3,2,1,0:T(2,128)(2,1)S(1)} %get-tuple-element.109), channel_id=1, source_target_pairs={{1,0},{2,1},{3,2},{5,4},{6,5},{7,6},{9,8},{10,9},{11,10},{13,12},{... | collective-permute-start | bytes 98312 | tf_op jit(solution)/shard_map/ppermute | solution.py:20
  40.1 6.1 %collective-permute-start.4 = (bf16[1,64,1,256]{3,2,1,0:T(2,128)(2,1)S(1)}, bf16[1,64,1,256]{3,2,1,0:T(2,128)(2,1)S(1)}, u32[]{:S(2)}, u32[]{:S(2)}) collective-permute-start(bf16[1,64,1,256]{3,2,1,0:T(2,128)(2,1)S(1)} %get-tuple-element.112), channel_id=1, source_target_pairs={{0,1},{1,2},{2,3},{4,5},{5,6},{6,7},{8,9},{9,10},{10,11},{12,13},{... | collective-permute-start | bytes 98312 | tf_op jit(solution)/shard_map/ppermute | solution.py:19
  44.3 4.4 %collective-permute-start.5 = (bf16[1,64,1,256]{3,2,1,0:T(2,128)(2,1)S(1)}, bf16[1,64,1,256]{3,2,1,0:T(2,128)(2,1)S(1)}, u32[]{:S(2)}, u32[]{:S(2)}) collective-permute-start(bf16[1,64,1,256]{3,2,1,0:T(2,128)(2,1)S(1)} %get-tuple-element.113), channel_id=1, source_target_pairs={{1,0},{2,1},{3,2},{5,4},{6,5},{7,6},{9,8},{10,9},{11,10},{13,12},{... | collective-permute-start | bytes 98312 | tf_op jit(solution)/shard_map/ppermute | solution.py:20
  66.5 10.7 %collective-permute-start.14 = (bf16[1,64,1,128]{1,3,2,0:T(8,128)(2,1)S(1)}, bf16[1,64,1,128]{1,3,2,0:T(8,128)(2,1)S(1)}, u32[]{:S(2)}, u32[]{:S(2)}) collective-permute-start(bf16[1,64,1,128]{1,3,2,0:T(8,128)(2,1)S(1)} %get-tuple-element.172), channel_id=1, source_target_pairs={{0,1},{1,2},{2,3},{4,5},{5,6},{6,7},{8,9},{9,10},{10,11},{12,13},{... | collective-permute-start | bytes 49160 | tf_op jit(solution)/shard_map/ppermute | solution.py:19
  71.4 5.8 %collective-permute-start.15 = (bf16[1,64,1,128]{1,3,2,0:T(8,128)(2,1)S(1)}, bf16[1,64,1,128]{1,3,2,0:T(8,128)(2,1)S(1)}, u32[]{:S(2)}, u32[]{:S(2)}) collective-permute-start(bf16[1,64,1,128]{1,3,2,0:T(8,128)(2,1)S(1)} %get-tuple-element.173), channel_id=1, source_target_pairs={{1,0},{2,1},{3,2},{5,4},{6,5},{7,6},{9,8},{10,9},{11,10},{13,12},{... | collective-permute-start | bytes 49160 | tf_op jit(solution)/shard_map/ppermute | solution.py:20
  72.8 4.9 %collective-permute-start.10 = (bf16[1,64,1,128]{1,3,2,0:T(8,128)(2,1)S(1)}, bf16[1,64,1,128]{1,3,2,0:T(8,128)(2,1)S(1)}, u32[]{:S(2)}, u32[]{:S(2)}) collective-permute-start(bf16[1,64,1,128]{1,3,2,0:T(8,128)(2,1)S(1)} %get-tuple-element.164), channel_id=1, source_target_pairs={{0,1},{1,2},{2,3},{4,5},{5,6},{6,7},{8,9},{9,10},{10,11},{12,13},{... | collective-permute-start | bytes 49160 | tf_op jit(solution)/shard_map/ppermute | solution.py:19
  75.9 3.9 %collective-permute-start.11 = (bf16[1,64,1,128]{1,3,2,0:T(8,128)(2,1)S(1)}, bf16[1,64,1,128]{1,3,2,0:T(8,128)(2,1)S(1)}, u32[]{:S(2)}, u32[]{:S(2)}) collective-permute-start(bf16[1,64,1,128]{1,3,2,0:T(8,128)(2,1)S(1)} %get-tuple-element.165), channel_id=1, source_target_pairs={{1,0},{2,1},{3,2},{5,4},{6,5},{7,6},{9,8},{10,9},{11,10},{13,12},{... | collective-permute-start | bytes 49160 | tf_op jit(solution)/shard_map/ppermute | solution.py:20
  83.6 10.2 %collective-permute-start.16 = (bf16[1,128,1,128]{1,3,2,0:T(8,128)(2,1)S(1)}, bf16[1,128,1,128]{1,3,2,0:T(8,128)(2,1)S(1)}, u32[]{:S(2)}, u32[]{:S(2)}) collective-permute-start(bf16[1,128,1,128]{1,3,2,0:T(8,128)(2,1)S(1)} %get-tuple-element.168), channel_id=1, source_target_pairs={{0,1},{1,2},{2,3},{4,5},{5,6},{6,7},{8,9},{9,10},{10,11},{12,13},{... | collective-permute-start | bytes 98312 | tf_op jit(solution)/shard_map/ppermute | solution.py:19
  88.1 5.7 %collective-permute-start.17 = (bf16[1,128,1,128]{1,3,2,0:T(8,128)(2,1)S(1)}, bf16[1,128,1,128]{1,3,2,0:T(8,128)(2,1)S(1)}, u32[]{:S(2)}, u32[]{:S(2)}) collective-permute-start(bf16[1,128,1,128]{1,3,2,0:T(8,128)(2,1)S(1)} %get-tuple-element.169), channel_id=1, source_target_pairs={{1,0},{2,1},{3,2},{5,4},{6,5},{7,6},{9,8},{10,9},{11,10},{13,12},{... | collective-permute-start | bytes 98312 | tf_op jit(solution)/shard_map/ppermute | solution.py:20
  89.5 5.7 %collective-permute-start.12 = (bf16[1,128,1,128]{1,3,2,0:T(8,128)(2,1)S(1)}, bf16[1,128,1,128]{1,3,2,0:T(8,128)(2,1)S(1)}, u32[]{:S(2)}, u32[]{:S(2)}) collective-permute-start(bf16[1,128,1,128]{1,3,2,0:T(8,128)(2,1)S(1)} %get-tuple-element.160), channel_id=1, source_target_pairs={{0,1},{1,2},{2,3},{4,5},{5,6},{6,7},{8,9},{9,10},{10,11},{12,13},{... | collective-permute-start | bytes 98312 | tf_op jit(solution)/shard_map/ppermute | solution.py:19
  92.5 3.9 %collective-permute-start.13 = (bf16[1,128,1,128]{1,3,2,0:T(8,128)(2,1)S(1)}, bf16[1,128,1,128]{1,3,2,0:T(8,128)(2,1)S(1)}, u32[]{:S(2)}, u32[]{:S(2)}) collective-permute-start(bf16[1,128,1,128]{1,3,2,0:T(8,128)(2,1)S(1)} %get-tuple-element.161), channel_id=1, source_target_pairs={{1,0},{2,1},{3,2},{5,4},{6,5},{7,6},{9,8},{10,9},{11,10},{13,12},{... | collective-permute-start | bytes 98312 | tf_op jit(solution)/shard_map/ppermute | solution.py:20
  100.3 8.0 %copy-start.8 = (bf16[128,128,3,3]{0,1,3,2:T(8,128)(2,1)S(1)}, bf16[128,128,3,3]{0,1,3,2:T(8,128)(2,1)}, u32[]{:S(2)}) copy-start(bf16[128,128,3,3]{0,1,3,2:T(8,128)(2,1)} %reverse_bitcast_fusion) | copy-start | bytes 884740
  100.4 6.0 %collective-permute-start.18 = (bf16[1,128,1,128]{1,3,2,0:T(8,128)(2,1)S(1)}, bf16[1,128,1,128]{1,3,2,0:T(8,128)(2,1)S(1)}, u32[]{:S(2)}, u32[]{:S(2)}) collective-permute-start(bf16[1,128,1,128]{1,3,2,0:T(8,128)(2,1)S(1)} %get-tuple-element.156), channel_id=1, source_target_pairs={{0,1},{1,2},{2,3},{4,5},{5,6},{6,7},{8,9},{9,10},{10,11},{12,13},{... | collective-permute-start | bytes 98312 | tf_op jit(solution)/shard_map/ppermute | solution.py:19
  105.1 3.1 %collective-permute-start.19 = (bf16[1,128,1,128]{1,3,2,0:T(8,128)(2,1)S(1)}, bf16[1,128,1,128]{1,3,2,0:T(8,128)(2,1)S(1)}, u32[]{:S(2)}, u32[]{:S(2)}) collective-permute-start(bf16[1,128,1,128]{1,3,2,0:T(8,128)(2,1)S(1)} %get-tuple-element.157), channel_id=1, source_target_pairs={{1,0},{2,1},{3,2},{5,4},{6,5},{7,6},{9,8},{10,9},{11,10},{13,12},{... | collective-permute-start | bytes 98312 | tf_op jit(solution)/shard_map/ppermute | solution.py:20
  110.3 7.5 %copy-start.9 = (f32[512,128]{1,0:T(8,128)}, f32[512,128]{1,0:T(8,128)S(1)}, u32[]{:S(2)}) copy-start(f32[512,128]{1,0:T(8,128)S(1)} %fusion.9) | copy-start | bytes 786436
  110.4 9.3 %collective-permute-start.20 = (bf16[1,128,1,128]{1,3,2,0:T(8,128)(2,1)S(1)}, bf16[1,128,1,128]{1,3,2,0:T(8,128)(2,1)S(1)}, u32[]{:S(2)}, u32[]{:S(2)}) collective-permute-start(bf16[1,128,1,128]{1,3,2,0:T(8,128)(2,1)S(1)} %get-tuple-element.152), channel_id=1, source_target_pairs={{0,1},{1,2},{2,3},{4,5},{5,6},{6,7},{8,9},{9,10},{10,11},{12,13},{... | collective-permute-start | bytes 98312 | tf_op jit(solution)/shard_map/ppermute | solution.py:19
  114.5 5.2 %collective-permute-start.21 = (bf16[1,128,1,128]{1,3,2,0:T(8,128)(2,1)S(1)}, bf16[1,128,1,128]{1,3,2,0:T(8,128)(2,1)S(1)}, u32[]{:S(2)}, u32[]{:S(2)}) collective-permute-start(bf16[1,128,1,128]{1,3,2,0:T(8,128)(2,1)S(1)} %get-tuple-element.153), channel_id=1, source_target_pairs={{1,0},{2,1},{3,2},{5,4},{6,5},{7,6},{9,8},{10,9},{11,10},{13,12},{... | collective-permute-start | bytes 98312 | tf_op jit(solution)/shard_map/ppermute | solution.py:20
  124.0 7.7 %copy-start.7 = (bf16[64,64,3,3]{1,0,3,2:T(8,128)(2,1)S(1)}, bf16[64,64,3,3]{1,0,3,2:T(8,128)(2,1)}, u32[]{:S(2)}) copy-start(bf16[64,64,3,3]{1,0,3,2:T(8,128)(2,1)} %param.29) | copy-start | bytes 221188
  126.7 7.8 %collective-permute-start.22 = (bf16[1,64,1,256]{3,2,1,0:T(2,128)(2,1)}, bf16[1,64,1,256]{3,2,1,0:T(2,128)(2,1)}, u32[]{:S(2)}, u32[]{:S(2)}) collective-permute-start(bf16[1,64,1,256]{3,2,1,0:T(2,128)(2,1)} %get-tuple-element.104), channel_id=1, source_target_pairs={{0,1},{1,2},{2,3},{4,5},{5,6},{6,7},{8,9},{9,10},{10,11},{12,13},{... | collective-permute-start | bytes 98312 | tf_op jit(solution)/shard_map/ppermute | solution.py:19
  130.4 5.0 %collective-permute-start.23 = (bf16[1,64,1,256]{3,2,1,0:T(2,128)(2,1)}, bf16[1,64,1,256]{3,2,1,0:T(2,128)(2,1)S(1)}, u32[]{:S(2)}, u32[]{:S(2)}) collective-permute-start(bf16[1,64,1,256]{3,2,1,0:T(2,128)(2,1)} %get-tuple-element.105), channel_id=1, source_target_pairs={{1,0},{2,1},{3,2},{5,4},{6,5},{7,6},{9,8},{10,9},{11,10},{13,12},{... | collective-permute-start | bytes 98312 | tf_op jit(solution)/shard_map/ppermute | solution.py:20
  141.2 4.8 %collective-permute-start.24 = (bf16[1,64,1,256]{3,2,1,0:T(2,128)(2,1)S(1)}, bf16[1,64,1,256]{3,2,1,0:T(2,128)(2,1)S(1)}, u32[]{:S(2)}, u32[]{:S(2)}) collective-permute-start(bf16[1,64,1,256]{3,2,1,0:T(2,128)(2,1)S(1)} %get-tuple-element.100), channel_id=1, source_target_pairs={{0,1},{1,2},{2,3},{4,5},{5,6},{6,7},{8,9},{9,10},{10,11},{12,13},{... | collective-permute-start | bytes 98312 | tf_op jit(solution)/shard_map/ppermute | solution.py:19
  144.5 4.2 %collective-permute-start.25 = (bf16[1,64,1,256]{3,2,1,0:T(2,128)(2,1)S(1)}, bf16[1,64,1,256]{3,2,1,0:T(2,128)(2,1)S(1)}, u32[]{:S(2)}, u32[]{:S(2)}) collective-permute-start(bf16[1,64,1,256]{3,2,1,0:T(2,128)(2,1)S(1)} %get-tuple-element.101), channel_id=1, source_target_pairs={{1,0},{2,1},{3,2},{5,4},{6,5},{7,6},{9,8},{10,9},{11,10},{13,12},{... | collective-permute-start | bytes 98312 | tf_op jit(solution)/shard_map/ppermute | solution.py:20
  151.5 7.7 %collective-permute-start.26 = (bf16[1,3,1,256]{3,1,2,0:T(4,128)(2,1)S(1)}, bf16[1,3,1,256]{3,1,2,0:T(4,128)(2,1)S(1)}, u32[]{:S(2)}, u32[]{:S(2)}) collective-permute-start(bf16[1,3,1,256]{3,1,2,0:T(4,128)(2,1)S(1)} %get-tuple-element.194), channel_id=1, source_target_pairs={{0,1},{1,2},{2,3},{4,5},{5,6},{6,7},{8,9},{9,10},{10,11},{12,13},{... | collective-permute-start | bytes 4616 | tf_op jit(solution)/shard_map/ppermute | solution.py:19
  156.4 3.1 %collective-permute-start.27 = (bf16[1,3,1,256]{3,1,2,0:T(4,128)(2,1)S(1)}, bf16[1,3,1,256]{3,1,2,0:T(4,128)(2,1)S(1)}, u32[]{:S(2)}, u32[]{:S(2)}) collective-permute-start(bf16[1,3,1,256]{3,1,2,0:T(4,128)(2,1)S(1)} %get-tuple-element.195), channel_id=1, source_target_pairs={{1,0},{2,1},{3,2},{5,4},{6,5},{7,6},{9,8},{10,9},{11,10},{13,12},{... | collective-permute-start | bytes 4616 | tf_op jit(solution)/shard_map/ppermute | solution.py:20
  (35 other events, 74.6 us)
where the time goes:
time: 210 us; the launch traced here: 208 us
  starting transfers between devices  75.1 us (36%)
  blocking collectives  41.5 us (20%)
  matrix products  32.7 us (16%)
  local copies, waits for them, and re-layouts  32.1 us (15%)
  other arithmetic  11.8 us (6%)
  waiting for transfers between devices  10.5 us (5%)
  between operations  4.34 us (2%)
    ppermute x13, starting transfers between devices, padded_2(): before = lax.ppermute(last, axis, up)  53.9 us
    psum x1, blocking collectives, local(): lax.psum((part_one + part_two, weight_grad, bias_grad), ('clip', 'row'))  41.5 us
    dot_general x126, matrix products, conv_valid(): jnp.dot(weight[:, :, row_shift, col_shift], piece.reshape(channels, row_c...  29.1 us
    ppermute x13, starting transfers between devices, padded_2(): after = lax.ppermute(leading, axis, down)  17.6 us
    unnamed x129, local copies, waits for them, and re-layouts  11.2 us
    ppermute x13, waiting for transfers between devices, padded_2(): after = lax.ppermute(leading, axis, down)  10.5 us
  transfers between devices with their start and end apart: 28, of which 7 were waited for; matrix products, arithmetic and copies ran while one was open for 10% of the time, Pallas kernels for 0%

commit v1 on v0

v1 whole, which is shorter than its diff:
```python
import math

import jax
import jax.numpy as jnp
from jax import lax
from jax.experimental import pallas as pl
from jax.experimental.pallas import tpu as pltpu
from jax.sharding import PartitionSpec as P

shift_values = [-0.03, -0.088, -0.188]
scale_values = [0.458, 0.448, 0.45]
PAD = 8
HALO = 6
F32 = jnp.float32
BF16 = jnp.bfloat16

erf_top = [0.00022905065861350646, 0.0034082910107109506, 0.050955695062380861, 0.18520832239976145, 1.128379143519084]
erf_bottom = [-1.1791602954361697e-7, 0.000023547966471313185, 0.0010179625278914885, 0.014070470171167667, 0.11098505178285362, 0.49746925110067538, 1.0]


def poly(x, coefs):
    total = jnp.full_like(x, coefs[0])
    for c in coefs[1:]:
        total = total * x + c
    return total


def phi(v):
    x = jnp.clip(v * (1.0 / math.sqrt(2.0)), -3.832506856900711, 3.832506856900711)
    sq = x * x
    return 0.5 + 0.5 * (x * poly(sq, erf_top) / poly(sq, erf_bottom))


def slope_of(v, cdf):
    return cdf + v * (jnp.exp(-0.5 * v * v) * (1.0 / math.sqrt(2.0 * math.pi)))


def dot(a, b):
    return jnp.dot(a, b, preferred_element_type=F32)


def left_right(x):
    width = x.shape[1]
    col = lax.broadcasted_iota(jnp.int32, x.shape, 1)
    left = jnp.where(col == 0, 0.0, pltpu.roll(x, 1, 1))
    right = jnp.where(col == width - 1, 0.0, pltpu.roll(x, width - 1, 1))
    return left, right


def put_taps(ref, where, x):
    c = x.shape[0]
    left, right = left_right(x)
    if c % 16:
        ref[where] = jnp.concatenate([left, x, right], 0).astype(BF16)
    else:
        ref[where + (slice(0, c),)] = left.astype(BF16)
        ref[where + (slice(c, 2 * c),)] = x.astype(BF16)
        ref[where + (slice(2 * c, 3 * c),)] = right.astype(BF16)


def fold_taps(y):
    n = y.shape[0] // 3
    width = y.shape[1]
    col = lax.broadcasted_iota(jnp.int32, (n, width), 1)
    left = jnp.where(col == 0, 0.0, pltpu.roll(y[:n], 1, 1))
    right = jnp.where(col == width - 1, 0.0, pltpu.roll(y[2 * n :], width - 1, 1))
    return left + y[n : 2 * n] + right


def conv_row(w_ref, x_ref, where, row):
    total = dot(w_ref[0], x_ref[where + (row,)])
    for a in (1, 2):
        total = total + dot(w_ref[a], x_ref[where + (row + a,)])
    return total


def two_parts(x):
    high = x.astype(BF16)
    low = (x - high.astype(F32)).astype(BF16)
    return high, low


def exact_dot(x, m):
    high, low = two_parts(x)
    return dot(high, m) + dot(low, m)


def lpips(dec, tgt, lin, count):
    inv_dec = 1.0 / jnp.sqrt(jnp.sum(dec * dec, 0, keepdims=True) + 1e-06)
    inv_tgt = 1.0 / jnp.sqrt(jnp.sum(tgt * tgt, 0, keepdims=True) + 1e-06)
    unit = dec * inv_dec
    differ = unit - tgt * inv_tgt
    weighted = lin * differ
    part = jnp.sum(weighted * differ, 0, keepdims=True) * (1.0 / count)
    grad = weighted * (2.0 / count)
    along = jnp.sum(grad * unit, 0, keepdims=True)
    return part, (grad - unit * along) * inv_dec


def channel_consts():
    o = lax.broadcasted_iota(jnp.int32, (PAD, 1), 0)

    def pick(values, other):
        out = jnp.full((PAD, 1), other, F32)
        for i, v in enumerate(values):
            out = jnp.where(o == i, v, out)
        return out

    return o, pick(shift_values, 0.0), pick(scale_values, 1.0)


def out_conv_kernel(f_ref, w_ref, own_ref, top_ref, bottom_ref):
    rows = f_ref.shape[0]
    width = f_ref.shape[2]
    folded = [fold_taps(dot(w_ref[...], f_ref[s])) for s in range(rows)]
    out = []
    for t in range(rows + 2):
        total = jnp.zeros((PAD, width), F32)
        for a in range(3):
            s = t + a - 2
            if 0 <= s < rows:
                total = total + folded[s][a * PAD : (a + 1) * PAD]
        out.append(total)
        own_ref[t] = total
    for k in range(HALO + 1):
        top_ref[k] = out[k]
        bottom_ref[k] = out[rows + 2 - (HALO + 1) + k]


def forward_kernel(
    start_ref, prev_ref, own_ref, next_ref, tprev_ref, town_ref, tnext_ref, ob_ref,
    w1_ref, b1_ref, w2_ref, b2_ref, w3_ref, b3_ref, w4_ref, b4_ref, l1_ref, l2_ref, pool_ref,
    s1_ref, gf_ref, s2_ref, s3_ref, g4_ref, loss_ref,
    x1, x2, x3, x4, part1, part2, *, height,
):
    rows = town_ref.shape[0]
    width = town_ref.shape[2]
    start = start_ref[0]
    o, shift, scale = channel_consts()

    def image(v, row):
        im = ((v.astype(BF16).astype(F32) - shift) / scale).astype(BF16).astype(F32)
        inside = jnp.logical_and(row >= 0, row < height)
        return jnp.where(jnp.logical_and(o < 3, inside), im, 0.0)

    for e in range(rows + 2 * HALO):
        v = jnp.zeros((PAD, width), F32)
        if HALO - 1 <= e < HALO + rows + 1:
            v = v + own_ref[e - HALO + 1]
        if e < HALO + 1:
            v = v + prev_ref[e]
        if e >= HALO + rows - 1:
            v = v + next_ref[e - (HALO + rows - 1)]
        put_taps(x1, (0, e), image(v + ob_ref[...], start + e - HALO))
        if e < HALO:
            tv = tprev_ref[e]
        elif e < HALO + rows:
            tv = town_ref[e - HALO]
        else:
            tv = tnext_ref[e - HALO - rows]
        put_taps(x1, (1, e), image(tv.astype(F32), start + e - HALO))

    def layer_one(q, carry):
        row = start + q - (HALO - 1)
        inside = jnp.logical_and(row >= 0, row < height)
        for im in range(2):
            pre = conv_row(w1_ref, x1, (im,), q) + b1_ref[...]
            cdf = phi(pre)
            put_taps(x2, (im, q), jnp.where(inside, pre * cdf, 0.0))
            if im == 0:
                s1_ref[q] = slope_of(pre, cdf)
        return carry

    lax.fori_loop(0, rows + 2 * HALO - 2, layer_one, 0)

    part1[...] = jnp.zeros_like(part1)
    part2[...] = jnp.zeros_like(part2)
    half = rows // 2
    edge = HALO - 4

    def layer_two(p, carry):
        row = start // 2 + p - edge
        inside = jnp.logical_and(row >= 0, row < height // 2)
        pres = [[conv_row(w2_ref, x2, (im,), 2 * p + k) + b2_ref[...] for k in range(2)] for im in range(2)]
        cdfs = [[phi(pres[im][k]) for k in range(2)] for im in range(2)]
        acts = [[pres[im][k] * cdfs[im][k] for k in range(2)] for im in range(2)]
        for im in range(2):
            pooled = exact_dot(acts[im][0] + acts[im][1], pool_ref[...])
            put_taps(x3, (im, p), jnp.where(inside, pooled, 0.0))

        @pl.when(jnp.logical_and(p >= edge, p < edge + half))
        def _():
            for k in range(2):
                part, grad = lpips(acts[0][k], acts[1][k], l1_ref[...], float(height * width))
                part1[...] += part
                gf_ref[2 * (p - edge) + k] = grad
                s2_ref[2 * (p - edge) + k] = slope_of(pres[0][k], cdfs[0][k])

        return carry

    lax.fori_loop(0, half + 2 * edge, layer_two, 0)

    def layer_three(t, carry):
        row = start // 2 + t - (edge - 1)
        inside = jnp.logical_and(row >= 0, row < height // 2)
        for im in range(2):
            pre = conv_row(w3_ref, x3, (im,), t) + b3_ref[...]
            cdf = phi(pre)
            put_taps(x4, (im, t), jnp.where(inside, pre * cdf, 0.0))
            if im == 0:
                s3_ref[t] = jnp.where(inside, slope_of(pre, cdf), 0.0)
        return carry

    lax.fori_loop(0, half + 2, layer_three, 0)

    def layer_four(u, carry):
        pres = [conv_row(w4_ref, x4, (im,), u) + b4_ref[...] for im in range(2)]
        cdfs = [phi(v) for v in pres]
        part, grad = lpips(
            pres[0] * cdfs[0], pres[1] * cdfs[1], l2_ref[...], float(height // 2 * (width // 2))
        )
        part2[...] += part
        g4_ref[u] = (grad * slope_of(pres[0], cdfs[0])).astype(BF16)
        return carry

    lax.fori_loop(0, half, layer_four, 0)
    loss_ref[...] = jnp.sum(part1[...], 1, keepdims=True) + jnp.sum(part2[...], 1, keepdims=True)


def deep_back_kernel(
    prev_ref, own_ref, next_ref, s3_ref, gf_ref, s2_ref, w4_ref, w3_ref, up_ref, g2_ref, x5, x6
):
    half = own_ref.shape[0]
    for e in range(half + 4):
        if e < 2:
            v = prev_ref[e]
        elif e < half + 2:
            v = own_ref[e - 2]
        else:
            v = next_ref[e - half - 2]
        put_taps(x5, (e,), v.astype(F32))

    def third(t, carry):
        put_taps(x6, (t,), conv_row(w4_ref, x5, (), t) * s3_ref[t])
        return carry

    lax.fori_loop(0, half + 2, third, 0)

    def second(p, carry):
        wide = exact_dot(conv_row(w3_ref, x6, (), p), up_ref[...])
        for k in range(2):
            g2_ref[2 * p + k] = ((gf_ref[2 * p + k] + wide) * s2_ref[2 * p + k]).astype(BF16)
        return carry

    lax.fori_loop(0, half, second, 0)


def shallow_back_kernel(
    start_ref, prev_ref, own_ref, next_ref, s1_ref, w2_ref, w1_ref, f_ref, loss_ref,
    taps_ref, sums_ref, x7, y, *, height,
):
    rows = own_ref.shape[0]
    start = start_ref[0]
    o, shift, scale = channel_consts()
    for e in range(rows + 6):
        if e < 3:
            v = prev_ref[e]
        elif e < rows + 3:
            v = own_ref[e - 3]
        else:
            v = next_ref[e - rows - 3]
        put_taps(x7, (e,), v.astype(F32))

    def first(q, carry):
        row = start + q - 2
        inside = jnp.logical_and(row >= 0, row < height)
        g1 = conv_row(w2_ref, x7, (), q) * s1_ref[q + HALO - 3]
        g1 = jnp.where(inside, g1, 0.0).astype(BF16)
        y[q] = fold_taps(dot(w1_ref[...], g1))
        return carry

    lax.fori_loop(0, rows + 4, first, 0)
    bias = jnp.zeros((PAD, 1), F32)
    for p in range(rows + 2):
        row = start + p - 1
        inside = jnp.logical_and(row >= 0, row < height)
        g = y[p, 0:PAD] + y[p + 1, PAD : 2 * PAD] + y[p + 2, 2 * PAD : 3 * PAD]
        g = jnp.where(inside, (g / scale).astype(BF16).astype(F32), 0.0)
        if 1 <= p <= rows:
            bias = bias + jnp.sum(g, 1, keepdims=True)
        put_taps(taps_ref, (p,), g)
    cf = f_ref.shape[1]
    for a in range(3):
        total = jnp.zeros((3 * PAD, cf), F32)
        for s in range(rows):
            total = total + lax.dot_general(
                taps_ref[s + 2 - a], f_ref[s], (((1,), (1,)), ((), ())), preferred_element_type=F32
            )
        sums_ref[a] = total
    last = jnp.where(o == 3, loss_ref[...], bias)
    sums_ref[3] = jnp.zeros((3 * PAD, cf), F32)
    sums_ref[3, 0:PAD] = jnp.broadcast_to(last, (PAD, cf))


def feature_kernel(taps_ref, w_ref, out_ref):
    for r in range(out_ref.shape[0]):
        out_ref[r] = conv_row(w_ref, taps_ref, (), r).astype(BF16)


def call(kernel, n_in, outs, scratch=(), smem=()):
    return pl.pallas_call(
        kernel,
        in_specs=[
            pl.BlockSpec(memory_space=pltpu.SMEM if i in smem else pltpu.VMEM) for i in range(n_in)
        ],
        out_specs=[pl.BlockSpec(memory_space=pltpu.VMEM) for _ in outs],
        out_shape=[jax.ShapeDtypeStruct(s, t) for s, t in outs],
        scratch_shapes=[pltpu.VMEM(s, t) for s, t in scratch],
        compiler_params=pltpu.CompilerParams(vmem_limit_bytes=48 * 1024 * 1024),
    )


def flipped(weight):
    return jnp.flip(weight, (2, 3)).transpose(1, 0, 2, 3)


def taps_in(w, pad=0):
    o, i = w.shape[:2]
    w = jnp.pad(w, ((0, 0), (0, pad), (0, 0), (0, 0)))
    return w.transpose(2, 0, 3, 1).reshape(3, o, 3 * (i + pad))


def taps_out(w):
    o, i = w.shape[:2]
    w = jnp.pad(w, ((0, PAD - o), (0, 0), (0, 0), (0, 0)))
    return w.transpose(3, 2, 0, 1).reshape(9 * PAD, i)


def from_neighbours(last, first):
    size = lax.axis_size("row")
    up = [(i, i + 1) for i in range(size - 1)]
    down = [(i + 1, i) for i in range(size - 1)]
    return lax.ppermute(last, "row", up), lax.ppermute(first, "row", down)


def local(
    features, out_weight, out_bias, targets, weight_one, bias_one, weight_two, bias_two,
    weight_three, bias_three, weight_four, bias_four, lin_one, lin_two,
):
    frames, cf, rows, width = features.shape
    c1 = weight_one.shape[0]
    c2 = weight_three.shape[0]
    assert frames == 1 and rows % 2 == 0 and rows > HALO
    height = rows * lax.axis_size("row")
    half, wh = rows // 2, width // 2
    edge = HALO - 4
    start = (lax.axis_index("row") * rows).astype(jnp.int32).reshape(1)

    tgt = jnp.pad(targets[0].transpose(1, 0, 2), ((0, 0), (0, PAD - targets.shape[1]), (0, 0)))
    tprev, tnext = from_neighbours(tgt[rows - HALO :], tgt[:HALO])
    feat = features[0].transpose(1, 0, 2)
    band = (HALO + 1, PAD, width)
    own, top, bottom = call(
        out_conv_kernel, 2, [((rows + 2, PAD, width), F32), (band, F32), (band, F32)]
    )(feat, taps_out(out_weight))
    prev, nxt = from_neighbours(bottom, top)

    j = jnp.arange(width)[:, None] // 2 == jnp.arange(wh)[None, :]
    pool = jnp.where(j, 0.25, 0.0).astype(BF16)
    col = lambda b: b[:, None]
    ob = jnp.pad(out_bias, (0, PAD - out_bias.shape[0]))

    r1 = rows + 2 * HALO
    s1, gf, s2, s3, g4, loss = call(
        lambda *r: forward_kernel(*r, height=height), 19,
        [
            ((r1 - 2, c1, width), F32), ((rows, c1, width), F32), ((rows, c1, width), F32),
            ((half + 2, c2, wh), F32), ((half, c2, wh), BF16), ((1, 1), F32),
        ],
        [
            ((2, r1, 3 * PAD, width), BF16), ((2, r1 - 2, 3 * c1, width), BF16),
            ((2, half + 2 * edge, 3 * c1, wh), BF16), ((2, half + 2, 3 * c2, wh), BF16),
            ((1, width), F32), ((1, wh), F32),
        ],
        smem=(0,),
    )(
        start, prev, own, nxt, tprev, tgt, tnext, col(ob),
        taps_in(weight_one, PAD - weight_one.shape[1]), col(bias_one), taps_in(weight_two), col(bias_two),
        taps_in(weight_three), col(bias_three), taps_in(weight_four), col(bias_four),
        col(lin_one), col(lin_two), pool,
    )

    gprev, gnext = from_neighbours(g4[half - 2 :], g4[:2])
    (g2,) = call(
        deep_back_kernel, 9, [((rows, c1, width), BF16)],
        [((half + 4, 3 * c2, wh), BF16), ((half + 2, 3 * c2, wh), BF16)],
    )(gprev, g4, gnext, s3, gf, s2, taps_in(flipped(weight_four)), taps_in(flipped(weight_three)), pool.T)

    g2prev, g2next = from_neighbours(g2[rows - 3 :], g2[:3])
    taps, sums = call(
        lambda *r: shallow_back_kernel(*r, height=height), 9,
        [((rows + 2, 3 * PAD, width), BF16), ((4, 3 * PAD, cf), F32)],
        [((rows + 6, 3 * c1, width), BF16), ((rows + 4, 3 * PAD, width), F32)],
        smem=(0,),
    )(start, g2prev, g2, g2next, s1, taps_in(flipped(weight_two)), taps_out(flipped(weight_one)), feat, loss)
    sums = lax.psum(sums, ("clip", "row"))
    (fg,) = call(feature_kernel, 2, [((rows, cf, width), BF16)])(
        taps, taps_in(flipped(out_weight), PAD - out_weight.shape[0])
    )
    feature_grad = fg.transpose(1, 0, 2)[None]
    wg = sums[:3].reshape(3, 3, PAD, cf)[:, ::-1, : out_weight.shape[0]].transpose(2, 3, 0, 1)
    return (sums[3, 3, 0], feature_grad, wg, sums[3, : out_weight.shape[0], 0])


def solution(mesh):
    tile = P("clip", None, "row", None)
    return jax.shard_map(
        local,
        mesh=mesh,
        in_specs=(tile, P(), P(), tile) + (P(),) * 10,
        out_specs=(P(), tile, P(), P()),
        check_vma=False,
    )
```

time: 210 us -> 110 us (0.52)
  starting transfers between devices: 75.1 us -> 21.8 us
  matrix products: 32.7 us -> 0 us
  Pallas kernels: 0 us -> 30.1 us
  local copies, waits for them, and re-layouts: 32.1 us -> 9.95 us
  other arithmetic: 11.8 us -> 0.12 us
  waiting for transfers between devices: 10.5 us -> 4.12 us
  between operations: 4.34 us -> 1.15 us
    ppermute x28 -> x8, starting transfers between devices: 75.1 us -> 21.8 us  [from_neighbours(): return (lax.ppermute(last, 'row', up), lax.ppermute(first, 'row', down))]
    dot_general x141 -> x0, matrix products: 32.7 us -> none  [the longest x126 29.1 us: conv_valid(): jnp.dot(weight[:, :, row_shift, col_shift], piece.reshape(channels, row_c...]
    pallas_call x0 -> x5, Pallas kernels: none -> 30.1 us  [the longest x1 19.3 us: local(): call(lambda *r: forward_kernel(*r, height=height), 19, [((r1 - 2, c1, wid...]
    unnamed x129 -> x37, local copies, waits for them, and re-layouts: 11.2 us -> 4.64 us
    ppermute x28 -> x8, waiting for transfers between devices: 10.5 us -> 4.12 us  [from_neighbours(): return (lax.ppermute(last, 'row', up), lax.ppermute(first, 'row', down))]
    slice x34 -> x6, local copies, waits for them, and re-layouts: 6.7 us -> 1.18 us  [the longest x2 1.14 us: local(): return (sums[3, 3, 0], feature_grad, wg, sums[3, :out_weight.shape[0], 0])]
    reduce_sum x3 -> x0, other arithmetic: 4.58 us -> none  [the longest x2 2.52 us: lpips_layer(): jnp.sum(grad_unit * unit_dec, 1, keepdims=True)]
    convert_element_type x12 -> x2, other arithmetic: 4.04 us -> 0.12 us  [local(): pool = jnp.where(j, 0.25, 0.0).astype(BF16)]
  transfers between devices with their start and end apart: 28 -> 8, of which waited for: 7 -> 2; matrix products, arithmetic and copies ran while one was open for 10% -> 3% of each run, Pallas kernels for 0% -> 0%
where the time goes in v1:
time: 110 us; the launch traced here: 109 us
  blocking collectives  42.1 us (38%)
  Pallas kernels  30.1 us (27%)
  starting transfers between devices  21.8 us (20%)
  local copies, waits for them, and re-layouts  9.95 us (9%)
  waiting for transfers between devices  4.12 us (4%)
  between operations  1.15 us (1%)
    psum x1, blocking collectives, local(): sums = lax.psum(sums, ('clip', 'row'))  42.1 us
    ppermute x8, starting transfers between devices, from_neighbours(): return (lax.ppermute(last, 'row', up), lax.ppermute(first, 'row', down))  21.8 us
    pallas_call x1, Pallas kernels, local(): call(lambda *r: forward_kernel(*r, height=height), 19, [((r1 - 2, c1, wid...  19.3 us
    pallas_call x1, Pallas kernels, local(): call(lambda *r: shallow_back_kernel(*r, height=height), 9, [((rows + 2, 3...  6.38 us
    unnamed x37, local copies, waits for them, and re-layouts  4.64 us
    ppermute x8, waiting for transfers between devices, from_neighbours(): return (lax.ppermute(last, 'row', up), lax.ppermute(first, 'row', down))  4.12 us
    pallas_call x1, Pallas kernels, local(): call(deep_back_kernel, 9, [((rows, c1, width), BF16)], [((half + 4, 3 * c...  3.54 us
  transfers between devices with their start and end apart: 8, of which 2 were waited for; matrix products, arithmetic and copies ran while one was open for 3% of the time, Pallas kernels for 0%

profile of v1, /device:TPU:0, one launch (start us, length us, event | category | flops | bytes accessed | tf_op | source)
XLA Modules:
  0.0 109.3 jit_solution(634217031280697067)
XLA Ops:
  0.7 1.2 %copy.69 = bf16[1,128,8,256]{3,1,2,0:T(8,128)(2,1)S(1)} copy(bf16[1,128,8,256]{3,2,1,0:T(8,128)(2,1)} %param.14) | data formatting | bytes 1048576 | tf_op args[0]
  1.9 0.7 pad_bitcast_fusion.1
  2.6 0.3 shard_map.165
  3.0 2.4 %collective-permute-start = (f32[7,8,256]{2,1,0:T(8,128)S(1)}, f32[7,8,256]{2,1,0:T(8,128)S(1)}, u32[]{:S(2)}, u32[]{:S(2)}) collective-permute-start(f32[7,8,256]{2,1,0:T(8,128)S(1)} %get-tuple-element.15), channel_id=1, source_target_pairs={{0,1},{1,2},{2,3},{4,5},{5,6},{6,7},{8,9},{9,10},{10,11},{12,13},{... | collective-permute-start | bytes 172040 | tf_op jit(solution)/shard_map/ppermute | solution.py:343
  5.4 1.3 %collective-permute-start.1 = (f32[7,8,256]{2,1,0:T(8,128)S(1)}, f32[7,8,256]{2,1,0:T(8,128)S(1)}, u32[]{:S(2)}, u32[]{:S(2)}) collective-permute-start(f32[7,8,256]{2,1,0:T(8,128)S(1)} %get-tuple-element.17), channel_id=1, source_target_pairs={{1,0},{2,1},{3,2},{5,4},{6,5},{7,6},{9,8},{10,9},{11,10},{13,12},{... | collective-permute-start | bytes 172040 | tf_op jit(solution)/shard_map/ppermute | solution.py:343
  6.7 5.1 %collective-permute-start.2 = (bf16[6,8,256]{2,1,0:T(8,128)(2,1)S(1)}, bf16[6,8,256]{2,1,0:T(8,128)(2,1)S(1)}, u32[]{:S(2)}, u32[]{:S(2)}) collective-permute-start(bf16[6,8,256]{2,1,0:T(8,128)(2,1)S(1)} %get-tuple-element.39), channel_id=1, source_target_pairs={{0,1},{1,2},{2,3},{4,5},{5,6},{6,7},{8,9},{9,10},{10,11},{12,13},{... | collective-permute-start | bytes 73736 | tf_op jit(solution)/shard_map/ppermute | solution.py:343
  11.9 1.3 %collective-permute-start.3 = (bf16[6,8,256]{2,1,0:T(8,128)(2,1)S(1)}, bf16[6,8,256]{2,1,0:T(8,128)(2,1)S(1)}, u32[]{:S(2)}, u32[]{:S(2)}) collective-permute-start(bf16[6,8,256]{2,1,0:T(8,128)(2,1)S(1)} %get-tuple-element.38), channel_id=1, source_target_pairs={{1,0},{2,1},{3,2},{5,4},{6,5},{7,6},{9,8},{10,9},{11,10},{13,12},{... | collective-permute-start | bytes 73736 | tf_op jit(solution)/shard_map/ppermute | solution.py:343
  13.5 0.2 copy.44
  13.8 0.6 copy.60
  14.4 0.2 copy.52.r_14_
  14.7 0.1 copy.43
  14.9 0.1 copy.48.r_10_
  15.0 0.1 copy.50.r_12_
  16.0 0.2 copy.57.w4_ref
  16.4 0.6 copy-done
  17.0 0.8 copy-done.1
  17.9 19.3 %shard_map.166 = (f32[18,64,256]{2,1,0:T(8,128)S(1)}, f32[8,64,256]{2,1,0:T(8,128)S(1)}, f32[8,64,256]{2,1,0:T(8,128)S(1)}, f32[6,128,128]{2,1,0:T(8,128)S(1)}, ...) custom-call(s32[1]{0:T(128)} %bitcast.r_0_, f32[7,8,256]{2,1,0:T(8,128)S(1)} %collective-permute-done.r_1_, ...), custom_call_target="tpu_custom_call" | custom-call | tf_op jit(solution)/shard_map/pallas_call | solution.py:374
  37.1 4.3 %collective-permute-start.4 = (bf16[2,128,128]{2,1,0:T(8,128)(2,1)S(1)}, bf16[2,128,128]{2,1,0:T(8,128)(2,1)S(1)}, u32[]{:S(2)}, u32[]{:S(2)}) collective-permute-start(bf16[2,128,128]{2,1,0:T(8,128)(2,1)S(1)} %get-tuple-element.37), channel_id=1, source_target_pairs={{0,1},{1,2},{2,3},{4,5},{5,6},{6,7},{8,9},{9,10},{10,11},{12,13},{... | collective-permute-start | bytes 196616 | tf_op jit(solution)/shard_map/ppermute | solution.py:343
  41.4 1.3 %collective-permute-start.5 = (bf16[2,128,128]{2,1,0:T(8,128)(2,1)S(1)}, bf16[2,128,128]{2,1,0:T(8,128)(2,1)S(1)}, u32[]{:S(2)}, u32[]{:S(2)}) collective-permute-start(bf16[2,128,128]{2,1,0:T(8,128)(2,1)S(1)} %get-tuple-element.36), channel_id=1, source_target_pairs={{1,0},{2,1},{3,2},{5,4},{6,5},{7,6},{9,8},{10,9},{11,10},{13,12},{... | collective-permute-start | bytes 196616 | tf_op jit(solution)/shard_map/ppermute | solution.py:343
  42.7 0.7 reverse_bitcast_fusion.1
  43.4 2.4 %collective-permute-done.5.next_ref = bf16[2,128,128]{2,1,0:T(8,128)(2,1)S(1)} collective-permute-done((bf16[2,128,128]{2,1,0:T(8,128)(2,1)S(1)}, bf16[2,128,128]{2,1,0:T(8,128)(2,1)S(1)}, u32[]{:S(2)}, u32[]{:S(2)}) %collective-permute-start.5) | collective-permute-done | bytes 65568 | tf_op jit(solution)/shard_map/ppermute | solution.py:343
  45.8 3.5 %shard_map.167.r_2_ = bf16[8,64,256]{2,1,0:T(8,128)(2,1)S(1)} custom-call(bf16[2,128,128]{2,1,0:T(8,128)(2,1)S(1)} %collective-permute-done.4.prev_ref, bf16[4,128,128]{2,1,0:T(8,128)(2,1)S(1)} %get-tuple-element.18.own_ref, bf16[2,128,128]{2,1,0:T(8,128)(2,1)S(1)} %collective-permute-done.5.next_ref, f32[6,128,128]{2,1,0:T(8,128)S(1)} %get-tuple-element.19.s3_ref, ...), custom_call_target="tpu_custom_call" | custom-call | tf_op jit(solution)/shard_map/pallas_call | solution.py:394
  49.4 4.8 %collective-permute-start.6 = (bf16[3,64,256]{2,1,0:T(8,128)(2,1)S(1)}, bf16[3,64,256]{2,1,0:T(8,128)(2,1)S(1)}, u32[]{:S(2)}, u32[]{:S(2)}) collective-permute-start(bf16[3,64,256]{2,1,0:T(8,128)(2,1)S(1)} %get-tuple-element.35), channel_id=1, source_target_pairs={{0,1},{1,2},{2,3},{4,5},{5,6},{6,7},{8,9},{9,10},{10,11},{12,13},{... | collective-permute-start | bytes 294920 | tf_op jit(solution)/shard_map/ppermute | solution.py:343
  54.2 1.3 %collective-permute-start.7 = (bf16[3,64,256]{2,1,0:T(8,128)(2,1)S(1)}, bf16[3,64,256]{2,1,0:T(8,128)(2,1)S(1)}, u32[]{:S(2)}, u32[]{:S(2)}) collective-permute-start(bf16[3,64,256]{2,1,0:T(8,128)(2,1)S(1)} %get-tuple-element.34), channel_id=1, source_target_pairs={{1,0},{2,1},{3,2},{5,4},{6,5},{7,6},{9,8},{10,9},{11,10},{13,12},{... | collective-permute-start | bytes 294920 | tf_op jit(solution)/shard_map/ppermute | solution.py:343
  55.7 1.7 %collective-permute-done.7.r_3_ = bf16[3,64,256]{2,1,0:T(8,128)(2,1)S(1)} collective-permute-done((bf16[3,64,256]{2,1,0:T(8,128)(2,1)S(1)}, bf16[3,64,256]{2,1,0:T(8,128)(2,1)S(1)}, u32[]{:S(2)}, u32[]{:S(2)}) %collective-permute-start.7) | collective-permute-done | bytes 98336 | tf_op jit(solution)/shard_map/ppermute | solution.py:343
  57.4 6.4 %shard_map.168 = (bf16[10,24,256]{2,1,0:T(8,128)(2,1)S(1)}, f32[4,24,128]{2,1,0:T(8,128)S(1)}) custom-call(s32[1]{0:T(128)} %bitcast.r_0_, bf16[3,64,256]{2,1,0:T(8,128)(2,1)S(1)} %collective-permute-done.6.r_1_, bf16[8,64,256]{2,1,0:T(8,128)(2,1)S(1)} %shard_map.167.r_2_, bf16[3,64,256]{2,1,0:T(8,128)(2,1)S(1)} %collective-permute-done.7.r_3_, ...), custom_call_target="tpu_custom_call" | custom-call | tf_op jit(solution)/shard_map/pallas_call | solution.py:400
  63.8 42.1 %psum.7 = f32[4,24,128]{2,1,0:T(8,128)S(1)} all-reduce(f32[4,24,128]{2,1,0:T(8,128)S(1)} %get-tuple-element.24), channel_id=1, replica_groups=mesh['clip'=8,'row'=4] {'clip','row'}, use_global_device_ids=true, to_apply=%region_0.1 | all-reduce | flops 12288 | bytes 98304 | tf_op jit(solution)/shard_map/psum | solution.py:406
  105.9 0.5 slice.42
  106.4 0.6 slice_reduce_fusion
  107.1 0.5 shard_map.169
  107.6 1.1 copy.63
  108.7 0.6 rev.28
  (66 shorter events, 1.5 us)
Async XLA Ops:
  0.6 6.1 %copy-start.7 = (bf16[1,3,8,256]{3,2,1,0:T(8,128)(2,1)S(1)}, bf16[1,3,8,256]{3,2,1,0:T(8,128)(2,1)}, u32[]{:S(2)}) copy-start(bf16[1,3,8,256]{3,2,1,0:T(8,128)(2,1)} %param.17) | copy-start | bytes 36868
  0.6 12.7 %copy-start.5 = (bf16[64,3,3,3]{0,3,2,1:T(4,128)(2,1)S(1)}, bf16[64,3,3,3]{0,3,2,1:T(4,128)(2,1)}, u32[]{:S(2)}) copy-start(bf16[64,3,3,3]{0,3,2,1:T(4,128)(2,1)} %param.18) | copy-start | bytes 10372
  0.7 12.8 %copy-start.4 = (bf16[128,64,3,3]{0,1,3,2:T(8,128)(2,1)S(1)}, bf16[128,64,3,3]{0,1,3,2:T(8,128)(2,1)}, u32[]{:S(2)}) copy-start(bf16[128,64,3,3]{0,1,3,2:T(8,128)(2,1)} %param.22) | copy-start | bytes 442372
  0.7 12.8 %copy-start.14 = (f32[3]{0:T(128)S(1)}, f32[3]{0:T(128)}, u32[]{:S(2)}) copy-start(f32[3]{0:T(128)} %param.16) | copy-start | bytes 40
  0.7 12.8 %copy-start.2 = (bf16[128,128,3,3]{1,0,3,2:T(8,128)(2,1)S(1)}, bf16[128,128,3,3]{1,0,3,2:T(8,128)(2,1)}, u32[]{:S(2)}) copy-start(bf16[128,128,3,3]{1,0,3,2:T(8,128)(2,1)} %param.24) | copy-start | bytes 884740
  2.6 11.2 %copy-start.6 = (bf16[3,128,3,3]{1,3,2,0:T(4,128)(2,1)S(1)}, bf16[3,128,3,3]{1,3,2,0:T(4,128)(2,1)}, u32[]{:S(2)}) copy-start(bf16[3,128,3,3]{1,3,2,0:T(4,128)(2,1)} %param.15) | copy-start | bytes 20740
  3.0 13.4 %collective-permute-start = (f32[7,8,256]{2,1,0:T(8,128)S(1)}, f32[7,8,256]{2,1,0:T(8,128)S(1)}, u32[]{:S(2)}, u32[]{:S(2)}) collective-permute-start(f32[7,8,256]{2,1,0:T(8,128)S(1)} %get-tuple-element.15), channel_id=1, source_target_pairs={{0,1},{1,2},{2,3},{4,5},{5,6},{6,7},{8,9},{9,10},{10,11},{12,13},{... | collective-permute-start | bytes 172040 | tf_op jit(solution)/shard_map/ppermute | solution.py:343
  5.4 11.0 %collective-permute-start.1 = (f32[7,8,256]{2,1,0:T(8,128)S(1)}, f32[7,8,256]{2,1,0:T(8,128)S(1)}, u32[]{:S(2)}, u32[]{:S(2)}) collective-permute-start(f32[7,8,256]{2,1,0:T(8,128)S(1)} %get-tuple-element.17), channel_id=1, source_target_pairs={{1,0},{2,1},{3,2},{5,4},{6,5},{7,6},{9,8},{10,9},{11,10},{13,12},{... | collective-permute-start | bytes 172040 | tf_op jit(solution)/shard_map/ppermute | solution.py:343
  6.7 9.6 %collective-permute-start.2 = (bf16[6,8,256]{2,1,0:T(8,128)(2,1)S(1)}, bf16[6,8,256]{2,1,0:T(8,128)(2,1)S(1)}, u32[]{:S(2)}, u32[]{:S(2)}) collective-permute-start(bf16[6,8,256]{2,1,0:T(8,128)(2,1)S(1)} %get-tuple-element.39), channel_id=1, source_target_pairs={{0,1},{1,2},{2,3},{4,5},{5,6},{6,7},{8,9},{9,10},{10,11},{12,13},{... | collective-permute-start | bytes 73736 | tf_op jit(solution)/shard_map/ppermute | solution.py:343
  11.9 4.5 %collective-permute-start.3 = (bf16[6,8,256]{2,1,0:T(8,128)(2,1)S(1)}, bf16[6,8,256]{2,1,0:T(8,128)(2,1)S(1)}, u32[]{:S(2)}, u32[]{:S(2)}) collective-permute-start(bf16[6,8,256]{2,1,0:T(8,128)(2,1)S(1)} %get-tuple-element.38), channel_id=1, source_target_pairs={{1,0},{2,1},{3,2},{5,4},{6,5},{7,6},{9,8},{10,9},{11,10},{13,12},{... | collective-permute-start | bytes 73736 | tf_op jit(solution)/shard_map/ppermute | solution.py:343
  13.2 1.5 %copy-start.3 = (bf16[64,64,3,3]{1,0,3,2:T(8,128)(2,1)S(1)}, bf16[64,64,3,3]{1,0,3,2:T(8,128)(2,1)}, u32[]{:S(2)}) copy-start(bf16[64,64,3,3]{1,0,3,2:T(8,128)(2,1)} %param.20) | copy-start | bytes 221188
  13.7 1.5 %copy-start.8 = (f32[128]{0:T(128)S(1)}, f32[128]{0:T(128)}, u32[]{:S(2)}) copy-start(f32[128]{0:T(128)} %param.23) | copy-start | bytes 1540
  13.7 1.6 %copy-start.9 = (f32[128]{0:T(128)S(1)}, f32[128]{0:T(128)}, u32[]{:S(2)}) copy-start(f32[128]{0:T(128)} %param.25) | copy-start | bytes 1540
  13.7 1.7 %copy-start.10 = (f32[128]{0:T(128)S(1)}, f32[128]{0:T(128)}, u32[]{:S(2)}) copy-start(f32[128]{0:T(128)} %param.27) | copy-start | bytes 1540
  13.8 1.8 %copy-start.11 = (f32[64]{0:T(128)S(1)}, f32[64]{0:T(128)}, u32[]{:S(2)}) copy-start(f32[64]{0:T(128)} %param.19) | copy-start | bytes 772
  13.8 1.9 %copy-start.12 = (f32[64]{0:T(128)S(1)}, f32[64]{0:T(128)}, u32[]{:S(2)}) copy-start(f32[64]{0:T(128)} %param.21) | copy-start | bytes 772
  13.8 2.0 %copy-start.13 = (f32[64]{0:T(128)S(1)}, f32[64]{0:T(128)}, u32[]{:S(2)}) copy-start(f32[64]{0:T(128)} %param.26) | copy-start | bytes 772
  16.4 0.6 copy-start
  17.0 0.8 copy-start.1
  37.1 6.3 %collective-permute-start.4 = (bf16[2,128,128]{2,1,0:T(8,128)(2,1)S(1)}, bf16[2,128,128]{2,1,0:T(8,128)(2,1)S(1)}, u32[]{:S(2)}, u32[]{:S(2)}) collective-permute-start(bf16[2,128,128]{2,1,0:T(8,128)(2,1)S(1)} %get-tuple-element.37), channel_id=1, source_target_pairs={{0,1},{1,2},{2,3},{4,5},{5,6},{6,7},{8,9},{9,10},{10,11},{12,13},{... | collective-permute-start | bytes 196616 | tf_op jit(solution)/shard_map/ppermute | solution.py:343
  41.4 4.4 %collective-permute-start.5 = (bf16[2,128,128]{2,1,0:T(8,128)(2,1)S(1)}, bf16[2,128,128]{2,1,0:T(8,128)(2,1)S(1)}, u32[]{:S(2)}, u32[]{:S(2)}) collective-permute-start(bf16[2,128,128]{2,1,0:T(8,128)(2,1)S(1)} %get-tuple-element.36), channel_id=1, source_target_pairs={{1,0},{2,1},{3,2},{5,4},{6,5},{7,6},{9,8},{10,9},{11,10},{13,12},{... | collective-permute-start | bytes 196616 | tf_op jit(solution)/shard_map/ppermute | solution.py:343
  49.4 6.3 %collective-permute-start.6 = (bf16[3,64,256]{2,1,0:T(8,128)(2,1)S(1)}, bf16[3,64,256]{2,1,0:T(8,128)(2,1)S(1)}, u32[]{:S(2)}, u32[]{:S(2)}) collective-permute-start(bf16[3,64,256]{2,1,0:T(8,128)(2,1)S(1)} %get-tuple-element.35), channel_id=1, source_target_pairs={{0,1},{1,2},{2,3},{4,5},{5,6},{6,7},{8,9},{9,10},{10,11},{12,13},{... | collective-permute-start | bytes 294920 | tf_op jit(solution)/shard_map/ppermute | solution.py:343
  54.2 3.2 %collective-permute-start.7 = (bf16[3,64,256]{2,1,0:T(8,128)(2,1)S(1)}, bf16[3,64,256]{2,1,0:T(8,128)(2,1)S(1)}, u32[]{:S(2)}, u32[]{:S(2)}) collective-permute-start(bf16[3,64,256]{2,1,0:T(8,128)(2,1)S(1)} %get-tuple-element.34), channel_id=1, source_target_pairs={{1,0},{2,1},{3,2},{5,4},{6,5},{7,6},{9,8},{10,9},{11,10},{13,12},{... | collective-permute-start | bytes 294920 | tf_op jit(solution)/shard_map/ppermute | solution.py:343

commit v2 on v1

--- a/solution.py
+++ b/solution.py
@@ -10,6 +10,7 @@
 shift_values = [-0.03, -0.088, -0.188]
 scale_values = [0.458, 0.448, 0.45]
 PAD = 8
+TGT = 4
 HALO = 6
 F32 = jnp.float32
 BF16 = jnp.bfloat16
@@ -103,13 +104,13 @@
     def pick(values, other):
         out = jnp.full((PAD, 1), other, F32)
         for i, v in enumerate(values):
-            out = jnp.where(o == i, v, out)
+            out = jnp.where(o % TGT == i, v, out)
         return out
 
     return o, pick(shift_values, 0.0), pick(scale_values, 1.0)
 
 
-def out_conv_kernel(f_ref, w_ref, own_ref, top_ref, bottom_ref):
+def out_conv_kernel(f_ref, w_ref, t_ref, own_ref, top_ref, bottom_ref):
     rows = f_ref.shape[0]
     width = f_ref.shape[2]
     folded = [fold_taps(dot(w_ref[...], f_ref[s])) for s in range(rows)]
@@ -120,6 +121,8 @@
             s = t + a - 2
             if 0 <= s < rows:
                 total = total + folded[s][a * PAD : (a + 1) * PAD]
+        if 1 <= t <= rows:
+            total = total + t_ref[t - 1]
         out.append(total)
         own_ref[t] = total
     for k in range(HALO + 1):
@@ -128,20 +131,20 @@
 
 
 def forward_kernel(
-    start_ref, prev_ref, own_ref, next_ref, tprev_ref, town_ref, tnext_ref, ob_ref,
+    start_ref, prev_ref, own_ref, next_ref, ob_ref,
     w1_ref, b1_ref, w2_ref, b2_ref, w3_ref, b3_ref, w4_ref, b4_ref, l1_ref, l2_ref, pool_ref,
     s1_ref, gf_ref, s2_ref, s3_ref, g4_ref, loss_ref,
     x1, x2, x3, x4, part1, part2, *, height,
 ):
-    rows = town_ref.shape[0]
-    width = town_ref.shape[2]
+    rows = own_ref.shape[0] - 2
+    width = own_ref.shape[2]
     start = start_ref[0]
     o, shift, scale = channel_consts()
 
     def image(v, row):
         im = ((v.astype(BF16).astype(F32) - shift) / scale).astype(BF16).astype(F32)
         inside = jnp.logical_and(row >= 0, row < height)
-        return jnp.where(jnp.logical_and(o < 3, inside), im, 0.0)
+        return jnp.where(jnp.logical_and(o % TGT < 3, inside), im, 0.0)
 
     for e in range(rows + 2 * HALO):
         v = jnp.zeros((PAD, width), F32)
@@ -151,20 +154,15 @@
             v = v + prev_ref[e]
         if e >= HALO + rows - 1:
             v = v + next_ref[e - (HALO + rows - 1)]
-        put_taps(x1, (0, e), image(v + ob_ref[...], start + e - HALO))
-        if e < HALO:
-            tv = tprev_ref[e]
-        elif e < HALO + rows:
-            tv = town_ref[e - HALO]
-        else:
-            tv = tnext_ref[e - HALO - rows]
-        put_taps(x1, (1, e), image(tv.astype(F32), start + e - HALO))
+        put_taps(x1, (e,), image(v + ob_ref[...], start + e - HALO))
 
     def layer_one(q, carry):
         row = start + q - (HALO - 1)
         inside = jnp.logical_and(row >= 0, row < height)
+        both = conv_row(w1_ref, x1, (), q)
+        c1 = b1_ref.shape[0]
         for im in range(2):
-            pre = conv_row(w1_ref, x1, (im,), q) + b1_ref[...]
+            pre = both[im * c1 : (im + 1) * c1] + b1_ref[...]
             cdf = phi(pre)
             put_taps(x2, (im, q), jnp.where(inside, pre * cdf, 0.0))
             if im == 0:
@@ -290,16 +288,18 @@
             bias = bias + jnp.sum(g, 1, keepdims=True)
         put_taps(taps_ref, (p,), g)
     cf = f_ref.shape[1]
+    totals = []
     for a in range(3):
         total = jnp.zeros((3 * PAD, cf), F32)
         for s in range(rows):
             total = total + lax.dot_general(
                 taps_ref[s + 2 - a], f_ref[s], (((1,), (1,)), ((), ())), preferred_element_type=F32
             )
-        sums_ref[a] = total
-    last = jnp.where(o == 3, loss_ref[...], bias)
-    sums_ref[3] = jnp.zeros((3 * PAD, cf), F32)
-    sums_ref[3, 0:PAD] = jnp.broadcast_to(last, (PAD, cf))
+        totals.append(total)
+    last = jnp.where(o == 7, loss_ref[...], pltpu.roll(jnp.broadcast_to(bias, (PAD, cf)), TGT, 0))
+    sums_ref[0] = totals[0] + pltpu.roll(totals[1], TGT, 0)
+    sums_ref[1] = totals[2]
+    sums_ref[1, 0:PAD] = totals[2][0:PAD] + last
 
 
 def feature_kernel(taps_ref, w_ref, out_ref):
@@ -334,6 +334,17 @@
     o, i = w.shape[:2]
     w = jnp.pad(w, ((0, PAD - o), (0, 0), (0, 0), (0, 0)))
     return w.transpose(3, 2, 0, 1).reshape(9 * PAD, i)
+
+
+def summed(array, axis):
+    size = lax.axis_size(axis)
+    if size & (size - 1):
+        return lax.psum(array, axis)
+    step = 1
+    while step < size:
+        array = array + lax.ppermute(array, axis, [(i, i ^ step) for i in range(size)])
+        step *= 2
+    return array
 
 
 def from_neighbours(last, first):
@@ -356,13 +367,14 @@
     edge = HALO - 4
     start = (lax.axis_index("row") * rows).astype(jnp.int32).reshape(1)
 
-    tgt = jnp.pad(targets[0].transpose(1, 0, 2), ((0, 0), (0, PAD - targets.shape[1]), (0, 0)))
-    tprev, tnext = from_neighbours(tgt[rows - HALO :], tgt[:HALO])
+    colors = targets.shape[1]
+    tgt = targets[0].astype(F32).transpose(1, 0, 2)
+    tgt = jnp.pad(tgt, ((0, 0), (TGT, PAD - TGT - colors), (0, 0)))
     feat = features[0].transpose(1, 0, 2)
     band = (HALO + 1, PAD, width)
     own, top, bottom = call(
-        out_conv_kernel, 2, [((rows + 2, PAD, width), F32), (band, F32), (band, F32)]
-    )(feat, taps_out(out_weight))
+        out_conv_kernel, 3, [((rows + 2, PAD, width), F32), (band, F32), (band, F32)]
+    )(feat, taps_out(out_weight), tgt)
     prev, nxt = from_neighbours(bottom, top)
 
     j = jnp.arange(width)[:, None] // 2 == jnp.arange(wh)[None, :]
@@ -370,22 +382,24 @@
     col = lambda b: b[:, None]
     ob = jnp.pad(out_bias, (0, PAD - out_bias.shape[0]))
 
+    w1 = jnp.pad(weight_one, ((0, 0), (0, PAD - colors), (0, 0), (0, 0)))
+    w1 = taps_in(jnp.concatenate([w1, jnp.roll(w1, TGT, 1)], 0))
     r1 = rows + 2 * HALO
     s1, gf, s2, s3, g4, loss = call(
-        lambda *r: forward_kernel(*r, height=height), 19,
+        lambda *r: forward_kernel(*r, height=height), 16,
         [
             ((r1 - 2, c1, width), F32), ((rows, c1, width), F32), ((rows, c1, width), F32),
             ((half + 2, c2, wh), F32), ((half, c2, wh), BF16), ((1, 1), F32),
         ],
         [
-            ((2, r1, 3 * PAD, width), BF16), ((2, r1 - 2, 3 * c1, width), BF16),
+            ((r1, 3 * PAD, width), BF16), ((2, r1 - 2, 3 * c1, width), BF16),
             ((2, half + 2 * edge, 3 * c1, wh), BF16), ((2, half + 2, 3 * c2, wh), BF16),
             ((1, width), F32), ((1, wh), F32),
         ],
         smem=(0,),
     )(
-        start, prev, own, nxt, tprev, tgt, tnext, col(ob),
-        taps_in(weight_one, PAD - weight_one.shape[1]), col(bias_one), taps_in(weight_two), col(bias_two),
+        start, prev, own, nxt, col(ob),
+        w1, col(bias_one), taps_in(weight_two), col(bias_two),
         taps_in(weight_three), col(bias_three), taps_in(weight_four), col(bias_four),
         col(lin_one), col(lin_two), pool,
     )
@@ -399,17 +413,20 @@
     g2prev, g2next = from_neighbours(g2[rows - 3 :], g2[:3])
     taps, sums = call(
         lambda *r: shallow_back_kernel(*r, height=height), 9,
-        [((rows + 2, 3 * PAD, width), BF16), ((4, 3 * PAD, cf), F32)],
+        [((rows + 2, 3 * PAD, width), BF16), ((2, 3 * PAD, cf), F32)],
         [((rows + 6, 3 * c1, width), BF16), ((rows + 4, 3 * PAD, width), F32)],
         smem=(0,),
     )(start, g2prev, g2, g2next, s1, taps_in(flipped(weight_two)), taps_out(flipped(weight_one)), feat, loss)
-    sums = lax.psum(sums, ("clip", "row"))
+    sums = summed(summed(sums, "row"), "clip")
     (fg,) = call(feature_kernel, 2, [((rows, cf, width), BF16)])(
         taps, taps_in(flipped(out_weight), PAD - out_weight.shape[0])
     )
     feature_grad = fg.transpose(1, 0, 2)[None]
-    wg = sums[:3].reshape(3, 3, PAD, cf)[:, ::-1, : out_weight.shape[0]].transpose(2, 3, 0, 1)
-    return (sums[3, 3, 0], feature_grad, wg, sums[3, : out_weight.shape[0], 0])
+    loss = sums[1, TGT + 3, 0]
+    bias_grad = sums[1, TGT : TGT + colors, 0]
+    sums = sums.reshape(2, 3, PAD, cf)[:, ::-1]
+    wg = jnp.stack([sums[0, :, :colors], sums[0, :, TGT : TGT + colors], sums[1, :, :colors]])
+    return (loss, feature_grad, wg.transpose(2, 3, 0, 1), bias_grad)
 
 
 def solution(mesh):

time: 110 us -> 79.1 us (0.72)
  blocking collectives: 42.1 us -> 0 us
  waiting for transfers between devices: 4.12 us -> 14.8 us
  starting transfers between devices: 21.8 us -> 24.6 us
  local copies, waits for them, and re-layouts: 9.95 us -> 7.37 us
    psum x1 -> x0, blocking collectives: 42.1 us -> none  [local(): sums = lax.psum(sums, ('clip', 'row'))]
    ppermute x0 -> x5, waiting for transfers between devices: none -> 9.46 us  [summed(): lax.ppermute(array, axis, [(i, i ^ step) for i in range(size)])]
    ppermute x0 -> x5, starting transfers between devices: none -> 8.6 us  [summed(): lax.ppermute(array, axis, [(i, i ^ step) for i in range(size)])]
    ppermute x8 -> x6, starting transfers between devices: 21.8 us -> 16 us  [from_neighbours(): return (lax.ppermute(last, 'row', up), lax.ppermute(first, 'row', down))]
    unnamed x37 -> x33, local copies, waits for them, and re-layouts: 4.64 us -> 3.3 us
    ppermute x8 -> x6, waiting for transfers between devices: 4.12 us -> 5.33 us  [from_neighbours(): return (lax.ppermute(last, 'row', up), lax.ppermute(first, 'row', down))]
  transfers between devices with their start and end apart: 8 -> 11, of which waited for: 2 -> 8; matrix products, arithmetic and copies ran while one was open for 3% -> 5% of each run, Pallas kernels for 0% -> 1%
where the time goes in v2:
time: 79.1 us; the launch traced here: 78.7 us
  Pallas kernels  30 us (38%)
  starting transfers between devices  24.6 us (31%)
  waiting for transfers between devices  14.8 us (19%)
  local copies, waits for them, and re-layouts  7.37 us (9%)
  between operations  1.04 us (1%)
  other arithmetic  0.85 us (1%)
    pallas_call x1, Pallas kernels, local(): call(lambda *r: forward_kernel(*r, height=height), 16, [((r1 - 2, c1, wid...  19.2 us
    ppermute x6, starting transfers between devices, from_neighbours(): return (lax.ppermute(last, 'row', up), lax.ppermute(first, 'row', down))  16 us
    ppermute x5, waiting for transfers between devices, summed(): lax.ppermute(array, axis, [(i, i ^ step) for i in range(size)])  9.46 us
    ppermute x5, starting transfers between devices, summed(): lax.ppermute(array, axis, [(i, i ^ step) for i in range(size)])  8.6 us
    pallas_call x1, Pallas kernels, local(): call(lambda *r: shallow_back_kernel(*r, height=height), 9, [((rows + 2, 3...  6.41 us
    ppermute x6, waiting for transfers between devices, from_neighbours(): return (lax.ppermute(last, 'row', up), lax.ppermute(first, 'row', down))  5.33 us
    pallas_call x1, Pallas kernels, local(): call(deep_back_kernel, 9, [((rows, c1, width), BF16)], [((half + 4, 3 * c...  3.54 us
    unnamed x33, local copies, waits for them, and re-layouts  3.3 us
  transfers between devices with their start and end apart: 11, of which 8 were waited for; matrix products, arithmetic and copies ran while one was open for 5% of the time, Pallas kernels for 1%

profile of v2, /device:TPU:0, one launch (start us, length us, event | category | flops | bytes accessed | tf_op | source)
XLA Modules:
  0.0 78.7 jit_solution(12391292354280042612)
XLA Ops:
  0.6 1.2 %copy.75 = bf16[1,128,8,256]{3,1,2,0:T(8,128)(2,1)S(1)} copy(bf16[1,128,8,256]{3,2,1,0:T(8,128)(2,1)} %param.14) | data formatting | bytes 1048576 | tf_op args[0]
  1.8 0.7 copy.76
  2.6 0.7 pad_bitcast_fusion.1
  3.3 0.3 shard_map.165
  3.6 2.5 %collective-permute-start = (f32[7,8,256]{2,1,0:T(8,128)S(1)}, f32[7,8,256]{2,1,0:T(8,128)S(1)}, u32[]{:S(2)}, u32[]{:S(2)}) collective-permute-start(f32[7,8,256]{2,1,0:T(8,128)S(1)} %get-tuple-element.15), channel_id=1, source_target_pairs={{0,1},{1,2},{2,3},{4,5},{5,6},{6,7},{8,9},{9,10},{10,11},{12,13},{... | collective-permute-start | bytes 172040 | tf_op jit(solution)/shard_map/ppermute | solution.py:354
  6.2 1.3 %collective-permute-start.1 = (f32[7,8,256]{2,1,0:T(8,128)S(1)}, f32[7,8,256]{2,1,0:T(8,128)S(1)}, u32[]{:S(2)}, u32[]{:S(2)}) collective-permute-start(f32[7,8,256]{2,1,0:T(8,128)S(1)} %get-tuple-element.17), channel_id=1, source_target_pairs={{1,0},{2,1},{3,2},{5,4},{6,5},{7,6},{9,8},{10,9},{11,10},{13,12},{... | collective-permute-start | bytes 172040 | tf_op jit(solution)/shard_map/ppermute | solution.py:354
  8.3 0.2 copy.54.r_11_
  9.7 0.2 copy.59.w4_ref
  10.1 1.3 %collective-permute-done.1.r_3_ = f32[7,8,256]{2,1,0:T(8,128)S(1)} collective-permute-done((f32[7,8,256]{2,1,0:T(8,128)S(1)}, f32[7,8,256]{2,1,0:T(8,128)S(1)}, u32[]{:S(2)}, u32[]{:S(2)}) %collective-permute-start.1) | collective-permute-done | bytes 57376 | tf_op jit(solution)/shard_map/ppermute | solution.py:354
  11.5 19.2 %shard_map.166 = (f32[18,64,256]{2,1,0:T(8,128)S(1)}, f32[8,64,256]{2,1,0:T(8,128)S(1)}, f32[8,64,256]{2,1,0:T(8,128)S(1)}, f32[6,128,128]{2,1,0:T(8,128)S(1)}, ...) custom-call(s32[1]{0:T(128)} %bitcast.r_0_, f32[7,8,256]{2,1,0:T(8,128)S(1)} %collective-permute-done.r_1_, ...), custom_call_target="tpu_custom_call" | custom-call | tf_op jit(solution)/shard_map/pallas_call | solution.py:388
  30.7 4.8 %collective-permute-start.2 = (bf16[2,128,128]{2,1,0:T(8,128)(2,1)S(1)}, bf16[2,128,128]{2,1,0:T(8,128)(2,1)S(1)}, u32[]{:S(2)}, u32[]{:S(2)}) collective-permute-start(bf16[2,128,128]{2,1,0:T(8,128)(2,1)S(1)} %get-tuple-element.37), channel_id=1, source_target_pairs={{0,1},{1,2},{2,3},{4,5},{5,6},{6,7},{8,9},{9,10},{10,11},{12,13},{... | collective-permute-start | bytes 196616 | tf_op jit(solution)/shard_map/ppermute | solution.py:354
  35.5 1.3 %collective-permute-start.3 = (bf16[2,128,128]{2,1,0:T(8,128)(2,1)S(1)}, bf16[2,128,128]{2,1,0:T(8,128)(2,1)S(1)}, u32[]{:S(2)}, u32[]{:S(2)}) collective-permute-start(bf16[2,128,128]{2,1,0:T(8,128)(2,1)S(1)} %get-tuple-element.36), channel_id=1, source_target_pairs={{1,0},{2,1},{3,2},{5,4},{6,5},{7,6},{9,8},{10,9},{11,10},{13,12},{... | collective-permute-start | bytes 196616 | tf_op jit(solution)/shard_map/ppermute | solution.py:354
  36.8 2.1 %collective-permute-done.3.next_ref = bf16[2,128,128]{2,1,0:T(8,128)(2,1)S(1)} collective-permute-done((bf16[2,128,128]{2,1,0:T(8,128)(2,1)S(1)}, bf16[2,128,128]{2,1,0:T(8,128)(2,1)S(1)}, u32[]{:S(2)}, u32[]{:S(2)}) %collective-permute-start.3) | collective-permute-done | bytes 65568 | tf_op jit(solution)/shard_map/ppermute | solution.py:354
  38.9 3.5 %shard_map.167.r_2_ = bf16[8,64,256]{2,1,0:T(8,128)(2,1)S(1)} custom-call(bf16[2,128,128]{2,1,0:T(8,128)(2,1)S(1)} %collective-permute-done.2.prev_ref, bf16[4,128,128]{2,1,0:T(8,128)(2,1)S(1)} %get-tuple-element.18.own_ref, bf16[2,128,128]{2,1,0:T(8,128)(2,1)S(1)} %collective-permute-done.3.next_ref, f32[6,128,128]{2,1,0:T(8,128)S(1)} %get-tuple-element.19.s3_ref, ...), custom_call_target="tpu_custom_call" | custom-call | tf_op jit(solution)/shard_map/pallas_call | solution.py:408
  42.5 4.8 %collective-permute-start.4 = (bf16[3,64,256]{2,1,0:T(8,128)(2,1)S(1)}, bf16[3,64,256]{2,1,0:T(8,128)(2,1)S(1)}, u32[]{:S(2)}, u32[]{:S(2)}) collective-permute-start(bf16[3,64,256]{2,1,0:T(8,128)(2,1)S(1)} %get-tuple-element.35), channel_id=1, source_target_pairs={{0,1},{1,2},{2,3},{4,5},{5,6},{6,7},{8,9},{9,10},{10,11},{12,13},{... | collective-permute-start | bytes 294920 | tf_op jit(solution)/shard_map/ppermute | solution.py:354
  47.4 1.3 %collective-permute-start.5 = (bf16[3,64,256]{2,1,0:T(8,128)(2,1)S(1)}, bf16[3,64,256]{2,1,0:T(8,128)(2,1)S(1)}, u32[]{:S(2)}, u32[]{:S(2)}) collective-permute-start(bf16[3,64,256]{2,1,0:T(8,128)(2,1)S(1)} %get-tuple-element.34), channel_id=1, source_target_pairs={{1,0},{2,1},{3,2},{5,4},{6,5},{7,6},{9,8},{10,9},{11,10},{13,12},{... | collective-permute-start | bytes 294920 | tf_op jit(solution)/shard_map/ppermute | solution.py:354
  48.7 1.9 %collective-permute-done.5.r_3_ = bf16[3,64,256]{2,1,0:T(8,128)(2,1)S(1)} collective-permute-done((bf16[3,64,256]{2,1,0:T(8,128)(2,1)S(1)}, bf16[3,64,256]{2,1,0:T(8,128)(2,1)S(1)}, u32[]{:S(2)}, u32[]{:S(2)}) %collective-permute-start.5) | collective-permute-done | bytes 98336 | tf_op jit(solution)/shard_map/ppermute | solution.py:354
  50.5 6.4 %shard_map.168 = (bf16[10,24,256]{2,1,0:T(8,128)(2,1)S(1)}, f32[2,24,128]{2,1,0:T(8,128)S(1)}) custom-call(s32[1]{0:T(128)} %bitcast.r_0_, bf16[3,64,256]{2,1,0:T(8,128)(2,1)S(1)} %collective-permute-done.4.r_1_, bf16[8,64,256]{2,1,0:T(8,128)(2,1)S(1)} %shard_map.167.r_2_, bf16[3,64,256]{2,1,0:T(8,128)(2,1)S(1)} %collective-permute-done.5.r_3_, ...), custom_call_target="tpu_custom_call" | custom-call | tf_op jit(solution)/shard_map/pallas_call | solution.py:414
  57.0 2.8 %collective-permute-start.6 = (f32[2,24,128]{2,1,0:T(8,128)S(1)}, f32[2,24,128]{2,1,0:T(8,128)S(1)}, u32[]{:S(2)}, u32[]{:S(2)}) collective-permute-start(f32[2,24,128]{2,1,0:T(8,128)S(1)} %get-tuple-element.24), channel_id=1, source_target_pairs={{0,1},{1,0},{2,3},{3,2},{4,5},{5,4},{6,7},{7,6},{8,9},{9,8},{10,11... | collective-permute-start | bytes 73736 | tf_op jit(solution)/shard_map/ppermute | solution.py:345
  59.8 0.8 %collective-permute-done.6 = f32[2,24,128]{2,1,0:T(8,128)S(1)} collective-permute-done((f32[2,24,128]{2,1,0:T(8,128)S(1)}, f32[2,24,128]{2,1,0:T(8,128)S(1)}, u32[]{:S(2)}, u32[]{:S(2)}) %collective-permute-start.6) | collective-permute-done | bytes 24608 | tf_op jit(solution)/shard_map/ppermute | solution.py:345
  60.8 3.7 %collective-permute-done.7 = f32[2,24,128]{2,1,0:T(8,128)S(1)} collective-permute-done((f32[2,24,128]{2,1,0:T(8,128)S(1)}, f32[2,24,128]{2,1,0:T(8,128)S(1)}, u32[]{:S(2)}, u32[]{:S(2)}) %collective-permute-start.7) | collective-permute-done | bytes 24608 | tf_op jit(solution)/shard_map/ppermute | solution.py:345
  64.4 1.5 %collective-permute-start.8 = (f32[2,24,128]{2,1,0:T(8,128)S(1)}, f32[2,24,128]{2,1,0:T(8,128)S(1)}, u32[]{:S(2)}, u32[]{:S(2)}) collective-permute-start(f32[2,24,128]{2,1,0:T(8,128)S(1)} %add.36), channel_id=1, source_target_pairs={{0,4},{4,0},{8,12},{12,8},{16,20},{20,16},{24,28},{28,24},{1,5},{5... | collective-permute-start | bytes 73736 | tf_op jit(solution)/shard_map/ppermute | solution.py:345
  65.9 2.3 %collective-permute-done.8 = f32[2,24,128]{2,1,0:T(8,128)S(1)} collective-permute-done((f32[2,24,128]{2,1,0:T(8,128)S(1)}, f32[2,24,128]{2,1,0:T(8,128)S(1)}, u32[]{:S(2)}, u32[]{:S(2)}) %collective-permute-start.8) | collective-permute-done | bytes 24608 | tf_op jit(solution)/shard_map/ppermute | solution.py:345
  68.3 1.6 %collective-permute-start.9 = (f32[2,24,128]{2,1,0:T(8,128)S(1)}, f32[2,24,128]{2,1,0:T(8,128)S(1)}, u32[]{:S(2)}, u32[]{:S(2)}) collective-permute-start(f32[2,24,128]{2,1,0:T(8,128)S(1)} %add.37), channel_id=1, source_target_pairs={{0,8},{4,12},{8,0},{12,4},{16,24},{20,28},{24,16},{28,20},{1,9},{5... | collective-permute-start | bytes 73736 | tf_op jit(solution)/shard_map/ppermute | solution.py:345
  69.9 2.2 %collective-permute-done.9 = f32[2,24,128]{2,1,0:T(8,128)S(1)} collective-permute-done((f32[2,24,128]{2,1,0:T(8,128)S(1)}, f32[2,24,128]{2,1,0:T(8,128)S(1)}, u32[]{:S(2)}, u32[]{:S(2)}) %collective-permute-start.9) | collective-permute-done | bytes 24608 | tf_op jit(solution)/shard_map/ppermute | solution.py:345
  72.1 2.6 %collective-permute-start.10 = (f32[2,24,128]{2,1,0:T(8,128)S(1)}, f32[2,24,128]{2,1,0:T(8,128)S(1)}, u32[]{:S(2)}, u32[]{:S(2)}) collective-permute-start(f32[2,24,128]{2,1,0:T(8,128)S(1)} %add.38), channel_id=1, source_target_pairs={{0,16},{4,20},{8,24},{12,28},{16,0},{20,4},{24,8},{28,12},{1,17},{... | collective-permute-start | bytes 73736 | tf_op jit(solution)/shard_map/ppermute | solution.py:345
  74.8 0.5 shard_map.169
  75.4 1.1 %copy.67 = bf16[1,128,8,256]{3,2,1,0:T(8,128)(2,1)} copy(bf16[1,128,8,256]{3,1,2,0:T(8,128)(2,1)S(1)} %bitcast.65) | data formatting | bytes 1048576
  76.5 0.4 collective-permute-done.10
  76.8 0.5 slice.57
  77.4 0.6 slice_reduce_fusion
  78.1 0.6 maximum_bitcast_fusion
  (75 shorter events, 2.5 us)
Async XLA Ops:
  0.6 7.0 %copy-start = (bf16[128,128,3,3]{1,0,3,2:T(8,128)(2,1)S(1)}, bf16[128,128,3,3]{1,0,3,2:T(8,128)(2,1)}, u32[]{:S(2)}) copy-start(bf16[128,128,3,3]{1,0,3,2:T(8,128)(2,1)} %param.24) | copy-start | bytes 884740
  1.8 6.1 %copy-start.3 = (bf16[64,3,3,3]{0,3,2,1:T(4,128)(2,1)S(1)}, bf16[64,3,3,3]{0,3,2,1:T(4,128)(2,1)}, u32[]{:S(2)}) copy-start(bf16[64,3,3,3]{0,3,2,1:T(4,128)(2,1)} %param.18) | copy-start | bytes 10372
  3.6 4.9 %copy-start.1 = (bf16[64,64,3,3]{1,0,3,2:T(8,128)(2,1)S(1)}, bf16[64,64,3,3]{1,0,3,2:T(8,128)(2,1)}, u32[]{:S(2)}) copy-start(bf16[64,64,3,3]{1,0,3,2:T(8,128)(2,1)} %param.20) | copy-start | bytes 221188
  3.6 6.5 %collective-permute-start = (f32[7,8,256]{2,1,0:T(8,128)S(1)}, f32[7,8,256]{2,1,0:T(8,128)S(1)}, u32[]{:S(2)}, u32[]{:S(2)}) collective-permute-start(f32[7,8,256]{2,1,0:T(8,128)S(1)} %get-tuple-element.15), channel_id=1, source_target_pairs={{0,1},{1,2},{2,3},{4,5},{5,6},{6,7},{8,9},{9,10},{10,11},{12,13},{... | collective-permute-start | bytes 172040 | tf_op jit(solution)/shard_map/ppermute | solution.py:354
  6.2 5.3 %collective-permute-start.1 = (f32[7,8,256]{2,1,0:T(8,128)S(1)}, f32[7,8,256]{2,1,0:T(8,128)S(1)}, u32[]{:S(2)}, u32[]{:S(2)}) collective-permute-start(f32[7,8,256]{2,1,0:T(8,128)S(1)} %get-tuple-element.17), channel_id=1, source_target_pairs={{1,0},{2,1},{3,2},{5,4},{6,5},{7,6},{9,8},{10,9},{11,10},{13,12},{... | collective-permute-start | bytes 172040 | tf_op jit(solution)/shard_map/ppermute | solution.py:354
  7.9 1.0 %copy-start.2 = (bf16[128,64,3,3]{0,1,3,2:T(8,128)(2,1)S(1)}, bf16[128,64,3,3]{0,1,3,2:T(8,128)(2,1)}, u32[]{:S(2)}) copy-start(bf16[128,64,3,3]{0,1,3,2:T(8,128)(2,1)} %param.22) | copy-start | bytes 442372
  7.9 1.1 %copy-start.5 = (f32[128]{0:T(128)S(1)}, f32[128]{0:T(128)}, u32[]{:S(2)}) copy-start(f32[128]{0:T(128)} %param.23) | copy-start | bytes 1540
  7.9 1.2 %copy-start.6 = (f32[128]{0:T(128)S(1)}, f32[128]{0:T(128)}, u32[]{:S(2)}) copy-start(f32[128]{0:T(128)} %param.25) | copy-start | bytes 1540
  7.9 1.3 %copy-start.7 = (f32[128]{0:T(128)S(1)}, f32[128]{0:T(128)}, u32[]{:S(2)}) copy-start(f32[128]{0:T(128)} %param.27) | copy-start | bytes 1540
  7.9 1.4 %copy-start.8 = (f32[64]{0:T(128)S(1)}, f32[64]{0:T(128)}, u32[]{:S(2)}) copy-start(f32[64]{0:T(128)} %param.19) | copy-start | bytes 772
  8.0 1.5 %copy-start.9 = (f32[64]{0:T(128)S(1)}, f32[64]{0:T(128)}, u32[]{:S(2)}) copy-start(f32[64]{0:T(128)} %param.21) | copy-start | bytes 772
  8.0 1.6 %copy-start.10 = (f32[64]{0:T(128)S(1)}, f32[64]{0:T(128)}, u32[]{:S(2)}) copy-start(f32[64]{0:T(128)} %param.26) | copy-start | bytes 772
  8.0 1.7 %copy-start.11 = (f32[3]{0:T(128)S(1)}, f32[3]{0:T(128)}, u32[]{:S(2)}) copy-start(f32[3]{0:T(128)} %param.16) | copy-start | bytes 40
  30.7 6.1 %collective-permute-start.2 = (bf16[2,128,128]{2,1,0:T(8,128)(2,1)S(1)}, bf16[2,128,128]{2,1,0:T(8,128)(2,1)S(1)}, u32[]{:S(2)}, u32[]{:S(2)}) collective-permute-start(bf16[2,128,128]{2,1,0:T(8,128)(2,1)S(1)} %get-tuple-element.37), channel_id=1, source_target_pairs={{0,1},{1,2},{2,3},{4,5},{5,6},{6,7},{8,9},{9,10},{10,11},{12,13},{... | collective-permute-start | bytes 196616 | tf_op jit(solution)/shard_map/ppermute | solution.py:354
  35.5 3.5 %collective-permute-start.3 = (bf16[2,128,128]{2,1,0:T(8,128)(2,1)S(1)}, bf16[2,128,128]{2,1,0:T(8,128)(2,1)S(1)}, u32[]{:S(2)}, u32[]{:S(2)}) collective-permute-start(bf16[2,128,128]{2,1,0:T(8,128)(2,1)S(1)} %get-tuple-element.36), channel_id=1, source_target_pairs={{1,0},{2,1},{3,2},{5,4},{6,5},{7,6},{9,8},{10,9},{11,10},{13,12},{... | collective-permute-start | bytes 196616 | tf_op jit(solution)/shard_map/ppermute | solution.py:354
  42.5 6.2 %collective-permute-start.4 = (bf16[3,64,256]{2,1,0:T(8,128)(2,1)S(1)}, bf16[3,64,256]{2,1,0:T(8,128)(2,1)S(1)}, u32[]{:S(2)}, u32[]{:S(2)}) collective-permute-start(bf16[3,64,256]{2,1,0:T(8,128)(2,1)S(1)} %get-tuple-element.35), channel_id=1, source_target_pairs={{0,1},{1,2},{2,3},{4,5},{5,6},{6,7},{8,9},{9,10},{10,11},{12,13},{... | collective-permute-start | bytes 294920 | tf_op jit(solution)/shard_map/ppermute | solution.py:354
  47.4 3.2 %collective-permute-start.5 = (bf16[3,64,256]{2,1,0:T(8,128)(2,1)S(1)}, bf16[3,64,256]{2,1,0:T(8,128)(2,1)S(1)}, u32[]{:S(2)}, u32[]{:S(2)}) collective-permute-start(bf16[3,64,256]{2,1,0:T(8,128)(2,1)S(1)} %get-tuple-element.34), channel_id=1, source_target_pairs={{1,0},{2,1},{3,2},{5,4},{6,5},{7,6},{9,8},{10,9},{11,10},{13,12},{... | collective-permute-start | bytes 294920 | tf_op jit(solution)/shard_map/ppermute | solution.py:354
  50.5 15.4 %copy-start.4 = (bf16[3,128,3,3]{1,3,2,0:T(4,128)(2,1)S(1)}, bf16[3,128,3,3]{1,3,2,0:T(4,128)(2,1)}, u32[]{:S(2)}) copy-start(bf16[3,128,3,3]{1,3,2,0:T(4,128)(2,1)} %param.15) | copy-start | bytes 20740
  57.0 3.6 %collective-permute-start.6 = (f32[2,24,128]{2,1,0:T(8,128)S(1)}, f32[2,24,128]{2,1,0:T(8,128)S(1)}, u32[]{:S(2)}, u32[]{:S(2)}) collective-permute-start(f32[2,24,128]{2,1,0:T(8,128)S(1)} %get-tuple-element.24), channel_id=1, source_target_pairs={{0,1},{1,0},{2,3},{3,2},{4,5},{5,4},{6,7},{7,6},{8,9},{9,8},{10,11... | collective-permute-start | bytes 73736 | tf_op jit(solution)/shard_map/ppermute | solution.py:345
  60.6 3.8 %collective-permute-start.7 = (f32[2,24,128]{2,1,0:T(8,128)S(1)}, f32[2,24,128]{2,1,0:T(8,128)S(1)}, u32[]{:S(2)}, u32[]{:S(2)}) collective-permute-start(f32[2,24,128]{2,1,0:T(8,128)S(1)} %add.35), channel_id=1, source_target_pairs={{0,2},{1,3},{2,0},{3,1},{4,6},{5,7},{6,4},{7,5},{8,10},{9,11},{10,... | collective-permute-start | bytes 73736 | tf_op jit(solution)/shard_map/ppermute | solution.py:345
  64.4 3.8 %collective-permute-start.8 = (f32[2,24,128]{2,1,0:T(8,128)S(1)}, f32[2,24,128]{2,1,0:T(8,128)S(1)}, u32[]{:S(2)}, u32[]{:S(2)}) collective-permute-start(f32[2,24,128]{2,1,0:T(8,128)S(1)} %add.36), channel_id=1, source_target_pairs={{0,4},{4,0},{8,12},{12,8},{16,20},{20,16},{24,28},{28,24},{1,5},{5... | collective-permute-start | bytes 73736 | tf_op jit(solution)/shard_map/ppermute | solution.py:345
  68.3 3.8 %collective-permute-start.9 = (f32[2,24,128]{2,1,0:T(8,128)S(1)}, f32[2,24,128]{2,1,0:T(8,128)S(1)}, u32[]{:S(2)}, u32[]{:S(2)}) collective-permute-start(f32[2,24,128]{2,1,0:T(8,128)S(1)} %add.37), channel_id=1, source_target_pairs={{0,8},{4,12},{8,0},{12,4},{16,24},{20,28},{24,16},{28,20},{1,9},{5... | collective-permute-start | bytes 73736 | tf_op jit(solution)/shard_map/ppermute | solution.py:345
  72.1 4.7 %collective-permute-start.10 = (f32[2,24,128]{2,1,0:T(8,128)S(1)}, f32[2,24,128]{2,1,0:T(8,128)S(1)}, u32[]{:S(2)}, u32[]{:S(2)}) collective-permute-start(f32[2,24,128]{2,1,0:T(8,128)S(1)} %add.38), channel_id=1, source_target_pairs={{0,16},{4,20},{8,24},{12,28},{16,0},{20,4},{24,8},{28,12},{1,17},{... | collective-permute-start | bytes 73736 | tf_op jit(solution)/shard_map/ppermute | solution.py:345

commit v3 on v2

--- a/solution.py
+++ b/solution.py
@@ -26,10 +26,15 @@
     return total
 
 
+LIMIT = 3.832506856900711 * math.sqrt(2.0)
+phi_top = [c * 0.5**k * 0.5 * math.sqrt(0.5) for k, c in zip(range(4, -1, -1), erf_top)]
+phi_bottom = [c * 0.5**k for k, c in zip(range(6, -1, -1), erf_bottom)]
+
+
 def phi(v):
-    x = jnp.clip(v * (1.0 / math.sqrt(2.0)), -3.832506856900711, 3.832506856900711)
+    x = jnp.clip(v, -LIMIT, LIMIT)
     sq = x * x
-    return 0.5 + 0.5 * (x * poly(sq, erf_top) / poly(sq, erf_bottom))
+    return 0.5 + x * poly(sq, phi_top) / poly(sq, phi_bottom)
 
 
 def slope_of(v, cdf):
@@ -132,9 +137,9 @@
 
 def forward_kernel(
     start_ref, prev_ref, own_ref, next_ref, ob_ref,
-    w1_ref, b1_ref, w2_ref, b2_ref, w3_ref, b3_ref, w4_ref, b4_ref, l1_ref, l2_ref, pool_ref,
-    s1_ref, gf_ref, s2_ref, s3_ref, g4_ref, loss_ref,
-    x1, x2, x3, x4, part1, part2, *, height,
+    w1_ref, b1_ref, w2_ref, b2_ref, w3_ref, b3_ref, w4_ref, b4_ref, l2_ref, pool_ref,
+    pre1_ref, cdf1_ref, pre2_ref, cdf2_ref, act2_ref, s3_ref, g4_ref, loss_ref,
+    x1, x2, x3, x4, part2, *, height,
 ):
     rows = own_ref.shape[0] - 2
     width = own_ref.shape[2]
@@ -166,12 +171,12 @@
             cdf = phi(pre)
             put_taps(x2, (im, q), jnp.where(inside, pre * cdf, 0.0))
             if im == 0:
-                s1_ref[q] = slope_of(pre, cdf)
+                pre1_ref[q] = pre
+                cdf1_ref[q] = cdf
         return carry
 
     lax.fori_loop(0, rows + 2 * HALO - 2, layer_one, 0)
 
-    part1[...] = jnp.zeros_like(part1)
     part2[...] = jnp.zeros_like(part2)
     half = rows // 2
     edge = HALO - 4
@@ -189,10 +194,9 @@
         @pl.when(jnp.logical_and(p >= edge, p < edge + half))
         def _():
             for k in range(2):
-                part, grad = lpips(acts[0][k], acts[1][k], l1_ref[...], float(height * width))
-                part1[...] += part
-                gf_ref[2 * (p - edge) + k] = grad
-                s2_ref[2 * (p - edge) + k] = slope_of(pres[0][k], cdfs[0][k])
+                pre2_ref[2 * (p - edge) + k] = pres[0][k]
+                cdf2_ref[2 * (p - edge) + k] = cdfs[0][k]
+                act2_ref[2 * (p - edge) + k] = acts[1][k]
 
         return carry
 
@@ -222,7 +226,32 @@
         return carry
 
     lax.fori_loop(0, half, layer_four, 0)
-    loss_ref[...] = jnp.sum(part1[...], 1, keepdims=True) + jnp.sum(part2[...], 1, keepdims=True)
+    loss_ref[...] = jnp.sum(part2[...], 1, keepdims=True)
+
+
+def block_one_kernel(
+    pre1_ref, cdf1_ref, pre2_ref, cdf2_ref, act2_ref, l1_ref, loss2_ref,
+    s1_ref, gf_ref, s2_ref, loss_ref, part1, *, count,
+):
+    rows = pre2_ref.shape[0]
+
+    def slopes(q, carry):
+        s1_ref[q] = slope_of(pre1_ref[q + HALO - 3], cdf1_ref[q + HALO - 3])
+        return carry
+
+    lax.fori_loop(0, rows + 4, slopes, 0)
+    part1[...] = jnp.zeros_like(part1)
+
+    def row(r, carry):
+        pre, cdf = pre2_ref[r], cdf2_ref[r]
+        part, grad = lpips(pre * cdf, act2_ref[r], l1_ref[...], count)
+        part1[...] += part
+        gf_ref[r] = grad
+        s2_ref[r] = slope_of(pre, cdf)
+        return carry
+
+    lax.fori_loop(0, rows, row, 0)
+    loss_ref[...] = jnp.sum(part1[...], 1, keepdims=True) + loss2_ref[...]
 
 
 def deep_back_kernel(
@@ -253,31 +282,39 @@
     lax.fori_loop(0, half, second, 0)
 
 
+def inner_back_kernel(own_ref, s1_ref, w2_ref, w1_ref, y_ref, x7):
+    rows = own_ref.shape[0]
+    for e in range(rows):
+        put_taps(x7, (e,), own_ref[e].astype(F32))
+
+    def first(k, carry):
+        g1 = (conv_row(w2_ref, x7, (), k) * s1_ref[k + 3]).astype(BF16)
+        y_ref[k] = fold_taps(dot(w1_ref[...], g1))
+        return carry
+
+    lax.fori_loop(0, rows - 2, first, 0)
+
+
 def shallow_back_kernel(
-    start_ref, prev_ref, own_ref, next_ref, s1_ref, w2_ref, w1_ref, f_ref, loss_ref,
+    start_ref, prev_ref, own_ref, next_ref, s1_ref, w2_ref, w1_ref, f_ref, loss_ref, inner_ref,
     taps_ref, sums_ref, x7, y, *, height,
 ):
     rows = own_ref.shape[0]
     start = start_ref[0]
     o, shift, scale = channel_consts()
-    for e in range(rows + 6):
-        if e < 3:
-            v = prev_ref[e]
-        elif e < rows + 3:
-            v = own_ref[e - 3]
-        else:
-            v = next_ref[e - rows - 3]
-        put_taps(x7, (e,), v.astype(F32))
-
-    def first(q, carry):
-        row = start + q - 2
-        inside = jnp.logical_and(row >= 0, row < height)
-        g1 = conv_row(w2_ref, x7, (), q) * s1_ref[q + HALO - 3]
-        g1 = jnp.where(inside, g1, 0.0).astype(BF16)
-        y[q] = fold_taps(dot(w1_ref[...], g1))
-        return carry
-
-    lax.fori_loop(0, rows + 4, first, 0)
+    for e in range(5):
+        put_taps(x7, (0, e), (prev_ref[e] if e < 3 else own_ref[e - 3]).astype(F32))
+        put_taps(x7, (1, e), (own_ref[rows - 2 + e] if e < 2 else next_ref[e - 2]).astype(F32))
+    for k in range(rows - 2):
+        y[k + 3] = inner_ref[k]
+    for side in range(2):
+        for k in range(3):
+            q = k + side * (rows + 1)
+            row = start + q - 2
+            inside = jnp.logical_and(row >= 0, row < height)
+            g1 = conv_row(w2_ref, x7, (side,), k) * s1_ref[q]
+            g1 = jnp.where(inside, g1, 0.0).astype(BF16)
+            y[q] = fold_taps(dot(w1_ref[...], g1))
     bias = jnp.zeros((PAD, 1), F32)
     for p in range(rows + 2):
         row = start + p - 1
@@ -385,38 +422,51 @@
     w1 = jnp.pad(weight_one, ((0, 0), (0, PAD - colors), (0, 0), (0, 0)))
     w1 = taps_in(jnp.concatenate([w1, jnp.roll(w1, TGT, 1)], 0))
     r1 = rows + 2 * HALO
-    s1, gf, s2, s3, g4, loss = call(
-        lambda *r: forward_kernel(*r, height=height), 16,
+    pre1, cdf1, pre2, cdf2, act2, s3, g4, loss = call(
+        lambda *r: forward_kernel(*r, height=height), 15,
         [
-            ((r1 - 2, c1, width), F32), ((rows, c1, width), F32), ((rows, c1, width), F32),
+            ((r1 - 2, c1, width), F32), ((r1 - 2, c1, width), F32),
+            ((rows, c1, width), F32), ((rows, c1, width), F32), ((rows, c1, width), F32),
             ((half + 2, c2, wh), F32), ((half, c2, wh), BF16), ((1, 1), F32),
         ],
         [
             ((r1, 3 * PAD, width), BF16), ((2, r1 - 2, 3 * c1, width), BF16),
             ((2, half + 2 * edge, 3 * c1, wh), BF16), ((2, half + 2, 3 * c2, wh), BF16),
-            ((1, width), F32), ((1, wh), F32),
+            ((1, wh), F32),
         ],
         smem=(0,),
     )(
         start, prev, own, nxt, col(ob),
         w1, col(bias_one), taps_in(weight_two), col(bias_two),
         taps_in(weight_three), col(bias_three), taps_in(weight_four), col(bias_four),
-        col(lin_one), col(lin_two), pool,
+        col(lin_two), pool,
     )
 
     gprev, gnext = from_neighbours(g4[half - 2 :], g4[:2])
+    s1, gf, s2, loss = call(
+        lambda *r: block_one_kernel(*r, count=float(height * width)), 7,
+        [
+            ((rows + 4, c1, width), F32), ((rows, c1, width), F32), ((rows, c1, width), F32),
+            ((1, 1), F32),
+        ],
+        [((1, width), F32)],
+    )(pre1, cdf1, pre2, cdf2, act2, col(lin_one), loss)
     (g2,) = call(
         deep_back_kernel, 9, [((rows, c1, width), BF16)],
         [((half + 4, 3 * c2, wh), BF16), ((half + 2, 3 * c2, wh), BF16)],
     )(gprev, g4, gnext, s3, gf, s2, taps_in(flipped(weight_four)), taps_in(flipped(weight_three)), pool.T)
 
     g2prev, g2next = from_neighbours(g2[rows - 3 :], g2[:3])
+    w2_back, w1_back = taps_in(flipped(weight_two)), taps_out(flipped(weight_one))
+    (inner,) = call(
+        inner_back_kernel, 4, [((rows - 2, 3 * PAD, width), F32)], [((rows, 3 * c1, width), BF16)]
+    )(g2, s1, w2_back, w1_back)
     taps, sums = call(
-        lambda *r: shallow_back_kernel(*r, height=height), 9,
+        lambda *r: shallow_back_kernel(*r, height=height), 10,
         [((rows + 2, 3 * PAD, width), BF16), ((2, 3 * PAD, cf), F32)],
-        [((rows + 6, 3 * c1, width), BF16), ((rows + 4, 3 * PAD, width), F32)],
+        [((2, 5, 3 * c1, width), BF16), ((rows + 4, 3 * PAD, width), F32)],
         smem=(0,),
-    )(start, g2prev, g2, g2next, s1, taps_in(flipped(weight_two)), taps_out(flipped(weight_one)), feat, loss)
+    )(start, g2prev, g2, g2next, s1, w2_back, w1_back, feat, loss, inner)
     sums = summed(summed(sums, "row"), "clip")
     (fg,) = call(feature_kernel, 2, [((rows, cf, width), BF16)])(
         taps, taps_in(flipped(out_weight), PAD - out_weight.shape[0])

time: 79.1 us -> 74.3 us (0.939)
  waiting for transfers between devices: 14.8 us -> 10.3 us
    ppermute x6, waiting for transfers between devices: 5.33 us -> 1.35 us  [from_neighbours(): return (lax.ppermute(last, 'row', up), lax.ppermute(first, 'row', down))]
    pallas_call x2 -> x4, Pallas kernels: 25.6 us -> 25.3 us  [the longest x1 17.8 us: local(): call(lambda *r: forward_kernel(*r, height=height), 15, [((r1 - 2, c1, wid...]
  transfers between devices with their start and end apart: 11 -> 11, of which waited for: 8 -> 6; matrix products, arithmetic and copies ran while one was open for 5% -> 5% of each run, Pallas kernels for 1% -> 7%
where the time goes in v3:
time: 74.3 us; the launch traced here: 73.9 us
  Pallas kernels  29.7 us (40%)
  starting transfers between devices  24.6 us (33%)
  waiting for transfers between devices  10.3 us (14%)
  local copies, waits for them, and re-layouts  7.37 us (10%)
  between operations  1.06 us (1%)
  other arithmetic  0.85 us (1%)
    pallas_call x1, Pallas kernels, local(): call(lambda *r: forward_kernel(*r, height=height), 15, [((r1 - 2, c1, wid...  17.8 us
    ppermute x6, starting transfers between devices, from_neighbours(): return (lax.ppermute(last, 'row', up), lax.ppermute(first, 'row', down))  15.8 us
    ppermute x5, waiting for transfers between devices, summed(): lax.ppermute(array, axis, [(i, i ^ step) for i in range(size)])  8.97 us
    ppermute x5, starting transfers between devices, summed(): lax.ppermute(array, axis, [(i, i ^ step) for i in range(size)])  8.72 us
    pallas_call x1, Pallas kernels, local(): call(deep_back_kernel, 9, [((rows, c1, width), BF16)], [((half + 4, 3 * c...  3.55 us
    unnamed x33, local copies, waits for them, and re-layouts  3.3 us
    pallas_call x1, Pallas kernels, local(): call(inner_back_kernel, 4, [((rows - 2, 3 * PAD, width), F32)], [((rows,...  2.59 us
    pallas_call x1, Pallas kernels, local(): call(lambda *r: shallow_back_kernel(*r, height=height), 10, [((rows + 2,...  2.56 us
  transfers between devices with their start and end apart: 11, of which 6 were waited for; matrix products, arithmetic and copies ran while one was open for 5% of the time, Pallas kernels for 7%

profile of v3, /device:TPU:0, one launch (start us, length us, event | category | flops | bytes accessed | tf_op | source)
XLA Modules:
  0.0 73.9 jit_solution(12691381765094049378)
XLA Ops:
  0.6 1.2 %copy.76 = bf16[1,128,8,256]{3,1,2,0:T(8,128)(2,1)S(1)} copy(bf16[1,128,8,256]{3,2,1,0:T(8,128)(2,1)} %param.14) | data formatting | bytes 1048576 | tf_op args[0]
  1.8 0.7 copy.77
  2.6 0.7 pad_bitcast_fusion.1
  3.3 0.3 shard_map.165
  3.6 2.5 %collective-permute-start = (f32[7,8,256]{2,1,0:T(8,128)S(1)}, f32[7,8,256]{2,1,0:T(8,128)S(1)}, u32[]{:S(2)}, u32[]{:S(2)}) collective-permute-start(f32[7,8,256]{2,1,0:T(8,128)S(1)} %get-tuple-element.21), channel_id=1, source_target_pairs={{0,1},{1,2},{2,3},{4,5},{5,6},{6,7},{8,9},{9,10},{10,11},{12,13},{... | collective-permute-start | bytes 172040 | tf_op jit(solution)/shard_map/ppermute | solution.py:391
  6.2 1.3 %collective-permute-start.1 = (f32[7,8,256]{2,1,0:T(8,128)S(1)}, f32[7,8,256]{2,1,0:T(8,128)S(1)}, u32[]{:S(2)}, u32[]{:S(2)}) collective-permute-start(f32[7,8,256]{2,1,0:T(8,128)S(1)} %get-tuple-element.23), channel_id=1, source_target_pairs={{1,0},{2,1},{3,2},{5,4},{6,5},{7,6},{9,8},{10,9},{11,10},{13,12},{... | collective-permute-start | bytes 172040 | tf_op jit(solution)/shard_map/ppermute | solution.py:391
  8.3 0.2 copy.54.r_11_
  10.1 1.3 %collective-permute-done.1.r_3_ = f32[7,8,256]{2,1,0:T(8,128)S(1)} collective-permute-done((f32[7,8,256]{2,1,0:T(8,128)S(1)}, f32[7,8,256]{2,1,0:T(8,128)S(1)}, u32[]{:S(2)}, u32[]{:S(2)}) %collective-permute-start.1) | collective-permute-done | bytes 57376 | tf_op jit(solution)/shard_map/ppermute | solution.py:391
  11.5 17.8 %shard_map.166 = (f32[18,64,256]{2,1,0:T(8,128)S(1)}, f32[18,64,256]{2,1,0:T(8,128)S(1)}, f32[8,64,256]{2,1,0:T(8,128)S(1)}, f32[8,64,256]{2,1,0:T(8,128)S(1)}, ...) custom-call(s32[1]{0:T(128)} %bitcast.r_0_, ...), custom_call_target="tpu_custom_call" | custom-call | tf_op jit(solution)/shard_map/pallas_call | solution.py:425
  29.3 4.8 %collective-permute-start.2 = (bf16[2,128,128]{2,1,0:T(8,128)(2,1)S(1)}, bf16[2,128,128]{2,1,0:T(8,128)(2,1)S(1)}, u32[]{:S(2)}, u32[]{:S(2)}) collective-permute-start(bf16[2,128,128]{2,1,0:T(8,128)(2,1)S(1)} %get-tuple-element.49), channel_id=1, source_target_pairs={{0,1},{1,2},{2,3},{4,5},{5,6},{6,7},{8,9},{9,10},{10,11},{12,13},{... | collective-permute-start | bytes 196616 | tf_op jit(solution)/shard_map/ppermute | solution.py:391
  34.1 1.3 %collective-permute-start.3 = (bf16[2,128,128]{2,1,0:T(8,128)(2,1)S(1)}, bf16[2,128,128]{2,1,0:T(8,128)(2,1)S(1)}, u32[]{:S(2)}, u32[]{:S(2)}) collective-permute-start(bf16[2,128,128]{2,1,0:T(8,128)(2,1)S(1)} %get-tuple-element.48), channel_id=1, source_target_pairs={{1,0},{2,1},{3,2},{5,4},{6,5},{7,6},{9,8},{10,9},{11,10},{13,12},{... | collective-permute-start | bytes 196616 | tf_op jit(solution)/shard_map/ppermute | solution.py:391
  35.4 2.3 %shard_map.167 = (f32[12,64,256]{2,1,0:T(8,128)S(1)}, f32[8,64,256]{2,1,0:T(8,128)S(1)}, f32[8,64,256]{2,1,0:T(8,128)S(1)}, f32[1,1]{1,0:T(1,128)}) custom-call(f32[18,64,256]{2,1,0:T(8,128)S(1)} %get-tuple-element.26.r_0_, f32[18,64,256]{2,1,0:T(8,128)S(1)} %get-tuple-element.27.r_1_, f32[8,64,256]{2,1,0:T(8,128)S(1)} %get-tuple-element.28.r_2_, ...), custom_call_target="tpu_custom_call" | custom-call | tf_op jit(solution)/shard_map/pallas_call | solution.py:446
  37.7 3.5 %shard_map.168.own_ref.r_2_ = bf16[8,64,256]{2,1,0:T(8,128)(2,1)S(1)} custom-call(bf16[2,128,128]{2,1,0:T(8,128)(2,1)S(1)} %collective-permute-done.2.prev_ref, bf16[4,128,128]{2,1,0:T(8,128)(2,1)S(1)} %get-tuple-element.24.own_ref, bf16[2,128,128]{2,1,0:T(8,128)(2,1)S(1)} %collective-permute-done.3.next_ref, f32[6,128,128]{2,1,0:T(8,128)S(1)} %get-tuple-element.25.s3_ref, ...), custom_call_target="tpu_custom_call" | custom-call | tf_op jit(solution)/shard_map/pallas_call | solution.py:454
  41.3 4.7 %collective-permute-start.4 = (bf16[3,64,256]{2,1,0:T(8,128)(2,1)S(1)}, bf16[3,64,256]{2,1,0:T(8,128)(2,1)S(1)}, u32[]{:S(2)}, u32[]{:S(2)}) collective-permute-start(bf16[3,64,256]{2,1,0:T(8,128)(2,1)S(1)} %get-tuple-element.47), channel_id=1, source_target_pairs={{0,1},{1,2},{2,3},{4,5},{5,6},{6,7},{8,9},{9,10},{10,11},{12,13},{... | collective-permute-start | bytes 294920 | tf_op jit(solution)/shard_map/ppermute | solution.py:391
  46.0 1.3 %collective-permute-start.5 = (bf16[3,64,256]{2,1,0:T(8,128)(2,1)S(1)}, bf16[3,64,256]{2,1,0:T(8,128)(2,1)S(1)}, u32[]{:S(2)}, u32[]{:S(2)}) collective-permute-start(bf16[3,64,256]{2,1,0:T(8,128)(2,1)S(1)} %get-tuple-element.46), channel_id=1, source_target_pairs={{1,0},{2,1},{3,2},{5,4},{6,5},{7,6},{9,8},{10,9},{11,10},{13,12},{... | collective-permute-start | bytes 294920 | tf_op jit(solution)/shard_map/ppermute | solution.py:391
  47.3 2.6 %shard_map.169.r_9_ = f32[6,24,256]{2,1,0:T(8,128)S(1)} custom-call(bf16[8,64,256]{2,1,0:T(8,128)(2,1)S(1)} %shard_map.168.own_ref.r_2_, f32[12,64,256]{2,1,0:T(8,128)S(1)} %get-tuple-element.34.s1_ref.r_4_, bf16[3,64,192]{2,1,0:T(8,128)(2,1)S(1)} %copy.62.w2_ref.r_5_, bf16[72,64]{1,0:T(8,128)(2,1)S(1)} %bitcast.66), custom_call_target="tpu_custom_call" | custom-call | tf_op jit(solution)/shard_map/pallas_call | solution.py:461
  50.0 2.6 %shard_map.170 = (bf16[10,24,256]{2,1,0:T(8,128)(2,1)S(1)}, f32[2,24,128]{2,1,0:T(8,128)S(1)}) custom-call(s32[1]{0:T(128)} %bitcast.r_0_, bf16[3,64,256]{2,1,0:T(8,128)(2,1)S(1)} %collective-permute-done.4.r_1_, bf16[8,64,256]{2,1,0:T(8,128)(2,1)S(1)} %shard_map.168.own_ref.r_2_, bf16[3,64,256]{2,1,0:T(8,128)(2,1)S(1)} %collective-permute-done.5.r_3_, ...), custom_call_target="tpu_custom_call" | custom-call | tf_op jit(solution)/shard_map/pallas_call | solution.py:464
  52.5 2.4 %collective-permute-start.6 = (f32[2,24,128]{2,1,0:T(8,128)S(1)}, f32[2,24,128]{2,1,0:T(8,128)S(1)}, u32[]{:S(2)}, u32[]{:S(2)}) collective-permute-start(f32[2,24,128]{2,1,0:T(8,128)S(1)} %get-tuple-element.36), channel_id=1, source_target_pairs={{0,1},{1,0},{2,3},{3,2},{4,5},{5,4},{6,7},{7,6},{8,9},{9,8},{10,11... | collective-permute-start | bytes 73736 | tf_op jit(solution)/shard_map/ppermute | solution.py:382
  54.9 0.8 %collective-permute-done.6 = f32[2,24,128]{2,1,0:T(8,128)S(1)} collective-permute-done((f32[2,24,128]{2,1,0:T(8,128)S(1)}, f32[2,24,128]{2,1,0:T(8,128)S(1)}, u32[]{:S(2)}, u32[]{:S(2)}) %collective-permute-start.6) | collective-permute-done | bytes 24608 | tf_op jit(solution)/shard_map/ppermute | solution.py:382
  55.8 0.6 collective-permute-start.7
  56.4 3.2 %collective-permute-done.7 = f32[2,24,128]{2,1,0:T(8,128)S(1)} collective-permute-done((f32[2,24,128]{2,1,0:T(8,128)S(1)}, f32[2,24,128]{2,1,0:T(8,128)S(1)}, u32[]{:S(2)}, u32[]{:S(2)}) %collective-permute-start.7) | collective-permute-done | bytes 24608 | tf_op jit(solution)/shard_map/ppermute | solution.py:382
  59.6 1.5 %collective-permute-start.8 = (f32[2,24,128]{2,1,0:T(8,128)S(1)}, f32[2,24,128]{2,1,0:T(8,128)S(1)}, u32[]{:S(2)}, u32[]{:S(2)}) collective-permute-start(f32[2,24,128]{2,1,0:T(8,128)S(1)} %add.36), channel_id=1, source_target_pairs={{0,4},{4,0},{8,12},{12,8},{16,20},{20,16},{24,28},{28,24},{1,5},{5... | collective-permute-start | bytes 73736 | tf_op jit(solution)/shard_map/ppermute | solution.py:382
  61.1 2.3 %collective-permute-done.8 = f32[2,24,128]{2,1,0:T(8,128)S(1)} collective-permute-done((f32[2,24,128]{2,1,0:T(8,128)S(1)}, f32[2,24,128]{2,1,0:T(8,128)S(1)}, u32[]{:S(2)}, u32[]{:S(2)}) %collective-permute-start.8) | collective-permute-done | bytes 24608 | tf_op jit(solution)/shard_map/ppermute | solution.py:382
  63.5 1.6 %collective-permute-start.9 = (f32[2,24,128]{2,1,0:T(8,128)S(1)}, f32[2,24,128]{2,1,0:T(8,128)S(1)}, u32[]{:S(2)}, u32[]{:S(2)}) collective-permute-start(f32[2,24,128]{2,1,0:T(8,128)S(1)} %add.37), channel_id=1, source_target_pairs={{0,8},{4,12},{8,0},{12,4},{16,24},{20,28},{24,16},{28,20},{1,9},{5... | collective-permute-start | bytes 73736 | tf_op jit(solution)/shard_map/ppermute | solution.py:382
  65.0 2.2 %collective-permute-done.9 = f32[2,24,128]{2,1,0:T(8,128)S(1)} collective-permute-done((f32[2,24,128]{2,1,0:T(8,128)S(1)}, f32[2,24,128]{2,1,0:T(8,128)S(1)}, u32[]{:S(2)}, u32[]{:S(2)}) %collective-permute-start.9) | collective-permute-done | bytes 24608 | tf_op jit(solution)/shard_map/ppermute | solution.py:382
  67.3 2.6 %collective-permute-start.10 = (f32[2,24,128]{2,1,0:T(8,128)S(1)}, f32[2,24,128]{2,1,0:T(8,128)S(1)}, u32[]{:S(2)}, u32[]{:S(2)}) collective-permute-start(f32[2,24,128]{2,1,0:T(8,128)S(1)} %add.38), channel_id=1, source_target_pairs={{0,16},{4,20},{8,24},{12,28},{16,0},{20,4},{24,8},{28,12},{1,17},{... | collective-permute-start | bytes 73736 | tf_op jit(solution)/shard_map/ppermute | solution.py:382
  70.0 0.5 shard_map.171
  70.6 1.1 %copy.68 = bf16[1,128,8,256]{3,2,1,0:T(8,128)(2,1)} copy(bf16[1,128,8,256]{3,1,2,0:T(8,128)(2,1)S(1)} %bitcast.65) | data formatting | bytes 1048576
  71.7 0.4 collective-permute-done.10
  72.0 0.5 slice.57
  72.5 0.6 slice_reduce_fusion
  73.3 0.6 maximum_bitcast_fusion
  (77 shorter events, 2.6 us)
Async XLA Ops:
  0.6 7.0 %copy-start = (bf16[128,128,3,3]{1,0,3,2:T(8,128)(2,1)S(1)}, bf16[128,128,3,3]{1,0,3,2:T(8,128)(2,1)}, u32[]{:S(2)}) copy-start(bf16[128,128,3,3]{1,0,3,2:T(8,128)(2,1)} %param.24) | copy-start | bytes 884740
  1.8 6.1 %copy-start.3 = (bf16[64,3,3,3]{0,3,2,1:T(4,128)(2,1)S(1)}, bf16[64,3,3,3]{0,3,2,1:T(4,128)(2,1)}, u32[]{:S(2)}) copy-start(bf16[64,3,3,3]{0,3,2,1:T(4,128)(2,1)} %param.18) | copy-start | bytes 10372
  3.6 4.9 %copy-start.1 = (bf16[64,64,3,3]{1,0,3,2:T(8,128)(2,1)S(1)}, bf16[64,64,3,3]{1,0,3,2:T(8,128)(2,1)}, u32[]{:S(2)}) copy-start(bf16[64,64,3,3]{1,0,3,2:T(8,128)(2,1)} %param.20) | copy-start | bytes 221188
  3.6 6.5 %collective-permute-start = (f32[7,8,256]{2,1,0:T(8,128)S(1)}, f32[7,8,256]{2,1,0:T(8,128)S(1)}, u32[]{:S(2)}, u32[]{:S(2)}) collective-permute-start(f32[7,8,256]{2,1,0:T(8,128)S(1)} %get-tuple-element.21), channel_id=1, source_target_pairs={{0,1},{1,2},{2,3},{4,5},{5,6},{6,7},{8,9},{9,10},{10,11},{12,13},{... | collective-permute-start | bytes 172040 | tf_op jit(solution)/shard_map/ppermute | solution.py:391
  6.2 5.3 %collective-permute-start.1 = (f32[7,8,256]{2,1,0:T(8,128)S(1)}, f32[7,8,256]{2,1,0:T(8,128)S(1)}, u32[]{:S(2)}, u32[]{:S(2)}) collective-permute-start(f32[7,8,256]{2,1,0:T(8,128)S(1)} %get-tuple-element.23), channel_id=1, source_target_pairs={{1,0},{2,1},{3,2},{5,4},{6,5},{7,6},{9,8},{10,9},{11,10},{13,12},{... | collective-permute-start | bytes 172040 | tf_op jit(solution)/shard_map/ppermute | solution.py:391
  7.9 1.0 %copy-start.2 = (bf16[128,64,3,3]{0,1,3,2:T(8,128)(2,1)S(1)}, bf16[128,64,3,3]{0,1,3,2:T(8,128)(2,1)}, u32[]{:S(2)}) copy-start(bf16[128,64,3,3]{0,1,3,2:T(8,128)(2,1)} %param.22) | copy-start | bytes 442372
  7.9 1.1 %copy-start.5 = (f32[128]{0:T(128)S(1)}, f32[128]{0:T(128)}, u32[]{:S(2)}) copy-start(f32[128]{0:T(128)} %param.23) | copy-start | bytes 1540
  7.9 1.2 %copy-start.6 = (f32[128]{0:T(128)S(1)}, f32[128]{0:T(128)}, u32[]{:S(2)}) copy-start(f32[128]{0:T(128)} %param.25) | copy-start | bytes 1540
  7.9 1.3 %copy-start.7 = (f32[128]{0:T(128)S(1)}, f32[128]{0:T(128)}, u32[]{:S(2)}) copy-start(f32[128]{0:T(128)} %param.27) | copy-start | bytes 1540
  7.9 1.4 %copy-start.8 = (f32[64]{0:T(128)S(1)}, f32[64]{0:T(128)}, u32[]{:S(2)}) copy-start(f32[64]{0:T(128)} %param.19) | copy-start | bytes 772
  8.0 1.5 %copy-start.9 = (f32[64]{0:T(128)S(1)}, f32[64]{0:T(128)}, u32[]{:S(2)}) copy-start(f32[64]{0:T(128)} %param.21) | copy-start | bytes 772
  8.0 1.6 %copy-start.11 = (f32[3]{0:T(128)S(1)}, f32[3]{0:T(128)}, u32[]{:S(2)}) copy-start(f32[3]{0:T(128)} %param.16) | copy-start | bytes 40
  8.0 1.7 %copy-start.10 = (f32[64]{0:T(128)S(1)}, f32[64]{0:T(128)}, u32[]{:S(2)}) copy-start(f32[64]{0:T(128)} %param.26) | copy-start | bytes 772
  29.3 8.4 %collective-permute-start.2 = (bf16[2,128,128]{2,1,0:T(8,128)(2,1)S(1)}, bf16[2,128,128]{2,1,0:T(8,128)(2,1)S(1)}, u32[]{:S(2)}, u32[]{:S(2)}) collective-permute-start(bf16[2,128,128]{2,1,0:T(8,128)(2,1)S(1)} %get-tuple-element.49), channel_id=1, source_target_pairs={{0,1},{1,2},{2,3},{4,5},{5,6},{6,7},{8,9},{9,10},{10,11},{12,13},{... | collective-permute-start | bytes 196616 | tf_op jit(solution)/shard_map/ppermute | solution.py:391
  34.1 3.7 %collective-permute-start.3 = (bf16[2,128,128]{2,1,0:T(8,128)(2,1)S(1)}, bf16[2,128,128]{2,1,0:T(8,128)(2,1)S(1)}, u32[]{:S(2)}, u32[]{:S(2)}) collective-permute-start(bf16[2,128,128]{2,1,0:T(8,128)(2,1)S(1)} %get-tuple-element.48), channel_id=1, source_target_pairs={{1,0},{2,1},{3,2},{5,4},{6,5},{7,6},{9,8},{10,9},{11,10},{13,12},{... | collective-permute-start | bytes 196616 | tf_op jit(solution)/shard_map/ppermute | solution.py:391
  41.3 8.6 %collective-permute-start.4 = (bf16[3,64,256]{2,1,0:T(8,128)(2,1)S(1)}, bf16[3,64,256]{2,1,0:T(8,128)(2,1)S(1)}, u32[]{:S(2)}, u32[]{:S(2)}) collective-permute-start(bf16[3,64,256]{2,1,0:T(8,128)(2,1)S(1)} %get-tuple-element.47), channel_id=1, source_target_pairs={{0,1},{1,2},{2,3},{4,5},{5,6},{6,7},{8,9},{9,10},{10,11},{12,13},{... | collective-permute-start | bytes 294920 | tf_op jit(solution)/shard_map/ppermute | solution.py:391
  46.0 4.0 %collective-permute-start.5 = (bf16[3,64,256]{2,1,0:T(8,128)(2,1)S(1)}, bf16[3,64,256]{2,1,0:T(8,128)(2,1)S(1)}, u32[]{:S(2)}, u32[]{:S(2)}) collective-permute-start(bf16[3,64,256]{2,1,0:T(8,128)(2,1)S(1)} %get-tuple-element.46), channel_id=1, source_target_pairs={{1,0},{2,1},{3,2},{5,4},{6,5},{7,6},{9,8},{10,9},{11,10},{13,12},{... | collective-permute-start | bytes 294920 | tf_op jit(solution)/shard_map/ppermute | solution.py:391
  49.9 11.2 %copy-start.4 = (bf16[3,128,3,3]{1,3,2,0:T(4,128)(2,1)S(1)}, bf16[3,128,3,3]{1,3,2,0:T(4,128)(2,1)}, u32[]{:S(2)}) copy-start(bf16[3,128,3,3]{1,3,2,0:T(4,128)(2,1)} %param.15) | copy-start | bytes 20740
  52.5 3.3 %collective-permute-start.6 = (f32[2,24,128]{2,1,0:T(8,128)S(1)}, f32[2,24,128]{2,1,0:T(8,128)S(1)}, u32[]{:S(2)}, u32[]{:S(2)}) collective-permute-start(f32[2,24,128]{2,1,0:T(8,128)S(1)} %get-tuple-element.36), channel_id=1, source_target_pairs={{0,1},{1,0},{2,3},{3,2},{4,5},{5,4},{6,7},{7,6},{8,9},{9,8},{10,11... | collective-permute-start | bytes 73736 | tf_op jit(solution)/shard_map/ppermute | solution.py:382
  55.8 3.8 %collective-permute-start.7 = (f32[2,24,128]{2,1,0:T(8,128)S(1)}, f32[2,24,128]{2,1,0:T(8,128)S(1)}, u32[]{:S(2)}, u32[]{:S(2)}) collective-permute-start(f32[2,24,128]{2,1,0:T(8,128)S(1)} %add.35), channel_id=1, source_target_pairs={{0,2},{1,3},{2,0},{3,1},{4,6},{5,7},{6,4},{7,5},{8,10},{9,11},{10,... | collective-permute-start | bytes 73736 | tf_op jit(solution)/shard_map/ppermute | solution.py:382
  59.6 3.8 %collective-permute-start.8 = (f32[2,24,128]{2,1,0:T(8,128)S(1)}, f32[2,24,128]{2,1,0:T(8,128)S(1)}, u32[]{:S(2)}, u32[]{:S(2)}) collective-permute-start(f32[2,24,128]{2,1,0:T(8,128)S(1)} %add.36), channel_id=1, source_target_pairs={{0,4},{4,0},{8,12},{12,8},{16,20},{20,16},{24,28},{28,24},{1,5},{5... | collective-permute-start | bytes 73736 | tf_op jit(solution)/shard_map/ppermute | solution.py:382
  63.5 3.8 %collective-permute-start.9 = (f32[2,24,128]{2,1,0:T(8,128)S(1)}, f32[2,24,128]{2,1,0:T(8,128)S(1)}, u32[]{:S(2)}, u32[]{:S(2)}) collective-permute-start(f32[2,24,128]{2,1,0:T(8,128)S(1)} %add.37), channel_id=1, source_target_pairs={{0,8},{4,12},{8,0},{12,4},{16,24},{20,28},{24,16},{28,20},{1,9},{5... | collective-permute-start | bytes 73736 | tf_op jit(solution)/shard_map/ppermute | solution.py:382
  67.3 4.7 %collective-permute-start.10 = (f32[2,24,128]{2,1,0:T(8,128)S(1)}, f32[2,24,128]{2,1,0:T(8,128)S(1)}, u32[]{:S(2)}, u32[]{:S(2)}) collective-permute-start(f32[2,24,128]{2,1,0:T(8,128)S(1)} %add.38), channel_id=1, source_target_pairs={{0,16},{4,20},{8,24},{12,28},{16,0},{20,4},{24,8},{28,12},{1,17},{... | collective-permute-start | bytes 73736 | tf_op jit(solution)/shard_map/ppermute | solution.py:382

commit v4 on v3

--- a/solution.py
+++ b/solution.py
@@ -175,7 +175,7 @@
                 cdf1_ref[q] = cdf
         return carry
 
-    lax.fori_loop(0, rows + 2 * HALO - 2, layer_one, 0)
+    lax.fori_loop(0, rows + 2 * HALO - 2, layer_one, 0, unroll=2)
 
     part2[...] = jnp.zeros_like(part2)
     half = rows // 2
@@ -200,7 +200,7 @@
 
         return carry
 
-    lax.fori_loop(0, half + 2 * edge, layer_two, 0)
+    lax.fori_loop(0, half + 2 * edge, layer_two, 0, unroll=2)
 
     def layer_three(t, carry):
         row = start // 2 + t - (edge - 1)
@@ -213,7 +213,7 @@
                 s3_ref[t] = jnp.where(inside, slope_of(pre, cdf), 0.0)
         return carry
 
-    lax.fori_loop(0, half + 2, layer_three, 0)
+    lax.fori_loop(0, half + 2, layer_three, 0, unroll=2)
 
     def layer_four(u, carry):
         pres = [conv_row(w4_ref, x4, (im,), u) + b4_ref[...] for im in range(2)]
@@ -225,7 +225,7 @@
         g4_ref[u] = (grad * slope_of(pres[0], cdfs[0])).astype(BF16)
         return carry
 
-    lax.fori_loop(0, half, layer_four, 0)
+    lax.fori_loop(0, half, layer_four, 0, unroll=2)
     loss_ref[...] = jnp.sum(part2[...], 1, keepdims=True)
 
 
@@ -239,7 +239,7 @@
         s1_ref[q] = slope_of(pre1_ref[q + HALO - 3], cdf1_ref[q + HALO - 3])
         return carry
 
-    lax.fori_loop(0, rows + 4, slopes, 0)
+    lax.fori_loop(0, rows + 4, slopes, 0, unroll=2)
     part1[...] = jnp.zeros_like(part1)
 
     def row(r, carry):
@@ -250,7 +250,7 @@
         s2_ref[r] = slope_of(pre, cdf)
         return carry
 
-    lax.fori_loop(0, rows, row, 0)
+    lax.fori_loop(0, rows, row, 0, unroll=2)
     loss_ref[...] = jnp.sum(part1[...], 1, keepdims=True) + loss2_ref[...]
 
 
@@ -271,7 +271,7 @@
         put_taps(x6, (t,), conv_row(w4_ref, x5, (), t) * s3_ref[t])
         return carry
 
-    lax.fori_loop(0, half + 2, third, 0)
+    lax.fori_loop(0, half + 2, third, 0, unroll=2)
 
     def second(p, carry):
         wide = exact_dot(conv_row(w3_ref, x6, (), p), up_ref[...])
@@ -279,7 +279,7 @@
             g2_ref[2 * p + k] = ((gf_ref[2 * p + k] + wide) * s2_ref[2 * p + k]).astype(BF16)
         return carry
 
-    lax.fori_loop(0, half, second, 0)
+    lax.fori_loop(0, half, second, 0, unroll=2)
 
 
 def inner_back_kernel(own_ref, s1_ref, w2_ref, w1_ref, y_ref, x7):
@@ -292,7 +292,7 @@
         y_ref[k] = fold_taps(dot(w1_ref[...], g1))
         return carry
 
-    lax.fori_loop(0, rows - 2, first, 0)
+    lax.fori_loop(0, rows - 2, first, 0, unroll=2)
 
 
 def shallow_back_kernel(

time: 74.3 us -> 70.2 us (0.945)
  Pallas kernels: 29.7 us -> 25.1 us
    pallas_call x1, Pallas kernels: 17.8 us -> 15.1 us  [local(): call(lambda *r: forward_kernel(*r, height=height), 15, [((r1 - 2, c1, wid...]
    pallas_call x1, Pallas kernels: 3.55 us -> 2.44 us  [local(): call(deep_back_kernel, 9, [((rows, c1, width), BF16)], [((half + 4, 3 * c...]
where the time goes in v4:
time: 70.2 us; the launch traced here: 69.8 us
  Pallas kernels  25.1 us (36%)
  starting transfers between devices  24.6 us (35%)
  waiting for transfers between devices  10.8 us (15%)
  local copies, waits for them, and re-layouts  7.37 us (10%)
  between operations  1.06 us (2%)
  other arithmetic  0.85 us (1%)
    ppermute x6, starting transfers between devices, from_neighbours(): return (lax.ppermute(last, 'row', up), lax.ppermute(first, 'row', down))  16 us
    pallas_call x1, Pallas kernels, local(): call(lambda *r: forward_kernel(*r, height=height), 15, [((r1 - 2, c1, wid...  15.1 us
    ppermute x5, waiting for transfers between devices, summed(): lax.ppermute(array, axis, [(i, i ^ step) for i in range(size)])  9.46 us
    ppermute x5, starting transfers between devices, summed(): lax.ppermute(array, axis, [(i, i ^ step) for i in range(size)])  8.54 us
    unnamed x33, local copies, waits for them, and re-layouts  3.3 us
    pallas_call x1, Pallas kernels, local(): call(lambda *r: shallow_back_kernel(*r, height=height), 10, [((rows + 2,...  2.56 us
    pallas_call x1, Pallas kernels, local(): call(deep_back_kernel, 9, [((rows, c1, width), BF16)], [((half + 4, 3 * c...  2.44 us
    pallas_call x1, Pallas kernels, local(): call(lambda *r: block_one_kernel(*r, count=float(height * width)), 7, [((...  2.1 us
  transfers between devices with their start and end apart: 11, of which 6 were waited for; matrix products, arithmetic and copies ran while one was open for 5% of the time, Pallas kernels for 7%

profile of v4, /device:TPU:0, one launch (start us, length us, event | category | flops | bytes accessed | tf_op | source)
XLA Modules:
  0.0 69.8 jit_solution(5035212582901910549)
XLA Ops:
  0.6 1.2 %copy.76 = bf16[1,128,8,256]{3,1,2,0:T(8,128)(2,1)S(1)} copy(bf16[1,128,8,256]{3,2,1,0:T(8,128)(2,1)} %param.14) | data formatting | bytes 1048576 | tf_op args[0]
  1.8 0.7 %copy.77 = bf16[1,3,8,256]{3,1,2,0:T(4,128)(2,1)S(1)} copy(bf16[1,3,8,256]{3,2,1,0:T(8,128)(2,1)} %param.17) | data formatting | bytes 24576 | tf_op args[3]
  2.6 0.7 %pad_bitcast_fusion.1 = bf16[3,3,8,128]{3,0,1,2:T(4,128)(2,1)S(1)} fusion(bf16[3,128,3,3]{1,3,2,0:T(4,128)(2,1)} %param.15), kind=kLoop, calls=%fused_computation.11 | loop fusion | bytes 25344 | tf_op jit(solution)/shard_map/transpose | solution.py:373
  3.3 0.3 shard_map.165
  3.6 2.5 %collective-permute-start = (f32[7,8,256]{2,1,0:T(8,128)S(1)}, f32[7,8,256]{2,1,0:T(8,128)S(1)}, u32[]{:S(2)}, u32[]{:S(2)}) collective-permute-start(f32[7,8,256]{2,1,0:T(8,128)S(1)} %get-tuple-element.21), channel_id=1, source_target_pairs={{0,1},{1,2},{2,3},{4,5},{5,6},{6,7},{8,9},{9,10},{10,11},{12,13},{... | collective-permute-start | bytes 172040 | tf_op jit(solution)/shard_map/ppermute | solution.py:391
  6.2 1.3 %collective-permute-start.1 = (f32[7,8,256]{2,1,0:T(8,128)S(1)}, f32[7,8,256]{2,1,0:T(8,128)S(1)}, u32[]{:S(2)}, u32[]{:S(2)}) collective-permute-start(f32[7,8,256]{2,1,0:T(8,128)S(1)} %get-tuple-element.23), channel_id=1, source_target_pairs={{1,0},{2,1},{3,2},{5,4},{6,5},{7,6},{9,8},{10,9},{11,10},{13,12},{... | collective-permute-start | bytes 172040 | tf_op jit(solution)/shard_map/ppermute | solution.py:391
  8.3 0.2 copy.54.r_11_
  9.7 0.2 copy.59.w4_ref
  10.1 1.3 %collective-permute-done.1.r_3_ = f32[7,8,256]{2,1,0:T(8,128)S(1)} collective-permute-done((f32[7,8,256]{2,1,0:T(8,128)S(1)}, f32[7,8,256]{2,1,0:T(8,128)S(1)}, u32[]{:S(2)}, u32[]{:S(2)}) %collective-permute-start.1) | collective-permute-done | bytes 57376 | tf_op jit(solution)/shard_map/ppermute | solution.py:391
  11.5 15.1 %shard_map.166 = (f32[18,64,256]{2,1,0:T(8,128)S(1)}, f32[18,64,256]{2,1,0:T(8,128)S(1)}, f32[8,64,256]{2,1,0:T(8,128)S(1)}, f32[8,64,256]{2,1,0:T(8,128)S(1)}, ...) custom-call(s32[1]{0:T(128)} %bitcast.r_0_, ...), custom_call_target="tpu_custom_call" | custom-call | tf_op jit(solution)/shard_map/pallas_call | solution.py:425
  26.5 4.8 %collective-permute-start.2 = (bf16[2,128,128]{2,1,0:T(8,128)(2,1)S(1)}, bf16[2,128,128]{2,1,0:T(8,128)(2,1)S(1)}, u32[]{:S(2)}, u32[]{:S(2)}) collective-permute-start(bf16[2,128,128]{2,1,0:T(8,128)(2,1)S(1)} %get-tuple-element.49), channel_id=1, source_target_pairs={{0,1},{1,2},{2,3},{4,5},{5,6},{6,7},{8,9},{9,10},{10,11},{12,13},{... | collective-permute-start | bytes 196616 | tf_op jit(solution)/shard_map/ppermute | solution.py:391
  31.3 1.3 %collective-permute-start.3 = (bf16[2,128,128]{2,1,0:T(8,128)(2,1)S(1)}, bf16[2,128,128]{2,1,0:T(8,128)(2,1)S(1)}, u32[]{:S(2)}, u32[]{:S(2)}) collective-permute-start(bf16[2,128,128]{2,1,0:T(8,128)(2,1)S(1)} %get-tuple-element.48), channel_id=1, source_target_pairs={{1,0},{2,1},{3,2},{5,4},{6,5},{7,6},{9,8},{10,9},{11,10},{13,12},{... | collective-permute-start | bytes 196616 | tf_op jit(solution)/shard_map/ppermute | solution.py:391
  32.6 2.1 %shard_map.167 = (f32[12,64,256]{2,1,0:T(8,128)S(1)}, f32[8,64,256]{2,1,0:T(8,128)S(1)}, f32[8,64,256]{2,1,0:T(8,128)S(1)}, f32[1,1]{1,0:T(1,128)}) custom-call(f32[18,64,256]{2,1,0:T(8,128)S(1)} %get-tuple-element.26.r_0_, f32[18,64,256]{2,1,0:T(8,128)S(1)} %get-tuple-element.27.r_1_, f32[8,64,256]{2,1,0:T(8,128)S(1)} %get-tuple-element.28.r_2_, ...), custom_call_target="tpu_custom_call" | custom-call | tf_op jit(solution)/shard_map/pallas_call | solution.py:446
  34.8 2.4 %shard_map.168.own_ref.r_2_ = bf16[8,64,256]{2,1,0:T(8,128)(2,1)S(1)} custom-call(bf16[2,128,128]{2,1,0:T(8,128)(2,1)S(1)} %collective-permute-done.2.prev_ref, bf16[4,128,128]{2,1,0:T(8,128)(2,1)S(1)} %get-tuple-element.24.own_ref, bf16[2,128,128]{2,1,0:T(8,128)(2,1)S(1)} %collective-permute-done.3.next_ref, f32[6,128,128]{2,1,0:T(8,128)S(1)} %get-tuple-element.25.s3_ref, ...), custom_call_target="tpu_custom_call" | custom-call | tf_op jit(solution)/shard_map/pallas_call | solution.py:454
  37.3 4.8 %collective-permute-start.4 = (bf16[3,64,256]{2,1,0:T(8,128)(2,1)S(1)}, bf16[3,64,256]{2,1,0:T(8,128)(2,1)S(1)}, u32[]{:S(2)}, u32[]{:S(2)}) collective-permute-start(bf16[3,64,256]{2,1,0:T(8,128)(2,1)S(1)} %get-tuple-element.47), channel_id=1, source_target_pairs={{0,1},{1,2},{2,3},{4,5},{5,6},{6,7},{8,9},{9,10},{10,11},{12,13},{... | collective-permute-start | bytes 294920 | tf_op jit(solution)/shard_map/ppermute | solution.py:391
  42.1 1.3 %collective-permute-start.5 = (bf16[3,64,256]{2,1,0:T(8,128)(2,1)S(1)}, bf16[3,64,256]{2,1,0:T(8,128)(2,1)S(1)}, u32[]{:S(2)}, u32[]{:S(2)}) collective-permute-start(bf16[3,64,256]{2,1,0:T(8,128)(2,1)S(1)} %get-tuple-element.46), channel_id=1, source_target_pairs={{1,0},{2,1},{3,2},{5,4},{6,5},{7,6},{9,8},{10,9},{11,10},{13,12},{... | collective-permute-start | bytes 294920 | tf_op jit(solution)/shard_map/ppermute | solution.py:391
  43.4 2.1 %shard_map.169.r_9_ = f32[6,24,256]{2,1,0:T(8,128)S(1)} custom-call(bf16[8,64,256]{2,1,0:T(8,128)(2,1)S(1)} %shard_map.168.own_ref.r_2_, f32[12,64,256]{2,1,0:T(8,128)S(1)} %get-tuple-element.34.s1_ref.r_4_, bf16[3,64,192]{2,1,0:T(8,128)(2,1)S(1)} %copy.62.w2_ref.r_5_, bf16[72,64]{1,0:T(8,128)(2,1)S(1)} %bitcast.66), custom_call_target="tpu_custom_call" | custom-call | tf_op jit(solution)/shard_map/pallas_call | solution.py:461
  45.6 2.6 %shard_map.170 = (bf16[10,24,256]{2,1,0:T(8,128)(2,1)S(1)}, f32[2,24,128]{2,1,0:T(8,128)S(1)}) custom-call(s32[1]{0:T(128)} %bitcast.r_0_, bf16[3,64,256]{2,1,0:T(8,128)(2,1)S(1)} %collective-permute-done.4.r_1_, bf16[8,64,256]{2,1,0:T(8,128)(2,1)S(1)} %shard_map.168.own_ref.r_2_, bf16[3,64,256]{2,1,0:T(8,128)(2,1)S(1)} %collective-permute-done.5.r_3_, ...), custom_call_target="tpu_custom_call" | custom-call | tf_op jit(solution)/shard_map/pallas_call | solution.py:464
  48.1 2.7 %collective-permute-start.6 = (f32[2,24,128]{2,1,0:T(8,128)S(1)}, f32[2,24,128]{2,1,0:T(8,128)S(1)}, u32[]{:S(2)}, u32[]{:S(2)}) collective-permute-start(f32[2,24,128]{2,1,0:T(8,128)S(1)} %get-tuple-element.36), channel_id=1, source_target_pairs={{0,1},{1,0},{2,3},{3,2},{4,5},{5,4},{6,7},{7,6},{8,9},{9,8},{10,11... | collective-permute-start | bytes 73736 | tf_op jit(solution)/shard_map/ppermute | solution.py:382
  50.8 0.8 %collective-permute-done.6 = f32[2,24,128]{2,1,0:T(8,128)S(1)} collective-permute-done((f32[2,24,128]{2,1,0:T(8,128)S(1)}, f32[2,24,128]{2,1,0:T(8,128)S(1)}, u32[]{:S(2)}, u32[]{:S(2)}) %collective-permute-start.6) | collective-permute-done | bytes 24608 | tf_op jit(solution)/shard_map/ppermute | solution.py:382
  51.9 3.7 %collective-permute-done.7 = f32[2,24,128]{2,1,0:T(8,128)S(1)} collective-permute-done((f32[2,24,128]{2,1,0:T(8,128)S(1)}, f32[2,24,128]{2,1,0:T(8,128)S(1)}, u32[]{:S(2)}, u32[]{:S(2)}) %collective-permute-start.7) | collective-permute-done | bytes 24608 | tf_op jit(solution)/shard_map/ppermute | solution.py:382
  55.5 1.5 %collective-permute-start.8 = (f32[2,24,128]{2,1,0:T(8,128)S(1)}, f32[2,24,128]{2,1,0:T(8,128)S(1)}, u32[]{:S(2)}, u32[]{:S(2)}) collective-permute-start(f32[2,24,128]{2,1,0:T(8,128)S(1)} %add.36), channel_id=1, source_target_pairs={{0,4},{4,0},{8,12},{12,8},{16,20},{20,16},{24,28},{28,24},{1,5},{5... | collective-permute-start | bytes 73736 | tf_op jit(solution)/shard_map/ppermute | solution.py:382
  57.0 2.3 %collective-permute-done.8 = f32[2,24,128]{2,1,0:T(8,128)S(1)} collective-permute-done((f32[2,24,128]{2,1,0:T(8,128)S(1)}, f32[2,24,128]{2,1,0:T(8,128)S(1)}, u32[]{:S(2)}, u32[]{:S(2)}) %collective-permute-start.8) | collective-permute-done | bytes 24608 | tf_op jit(solution)/shard_map/ppermute | solution.py:382
  59.4 1.6 %collective-permute-start.9 = (f32[2,24,128]{2,1,0:T(8,128)S(1)}, f32[2,24,128]{2,1,0:T(8,128)S(1)}, u32[]{:S(2)}, u32[]{:S(2)}) collective-permute-start(f32[2,24,128]{2,1,0:T(8,128)S(1)} %add.37), channel_id=1, source_target_pairs={{0,8},{4,12},{8,0},{12,4},{16,24},{20,28},{24,16},{28,20},{1,9},{5... | collective-permute-start | bytes 73736 | tf_op jit(solution)/shard_map/ppermute | solution.py:382
  61.0 2.2 %collective-permute-done.9 = f32[2,24,128]{2,1,0:T(8,128)S(1)} collective-permute-done((f32[2,24,128]{2,1,0:T(8,128)S(1)}, f32[2,24,128]{2,1,0:T(8,128)S(1)}, u32[]{:S(2)}, u32[]{:S(2)}) %collective-permute-start.9) | collective-permute-done | bytes 24608 | tf_op jit(solution)/shard_map/ppermute | solution.py:382
  63.2 2.6 %collective-permute-start.10 = (f32[2,24,128]{2,1,0:T(8,128)S(1)}, f32[2,24,128]{2,1,0:T(8,128)S(1)}, u32[]{:S(2)}, u32[]{:S(2)}) collective-permute-start(f32[2,24,128]{2,1,0:T(8,128)S(1)} %add.38), channel_id=1, source_target_pairs={{0,16},{4,20},{8,24},{12,28},{16,0},{20,4},{24,8},{28,12},{1,17},{... | collective-permute-start | bytes 73736 | tf_op jit(solution)/shard_map/ppermute | solution.py:382
  65.9 0.5 shard_map.171
  66.5 1.1 %copy.68 = bf16[1,128,8,256]{3,2,1,0:T(8,128)(2,1)} copy(bf16[1,128,8,256]{3,1,2,0:T(8,128)(2,1)S(1)} %bitcast.65) | data formatting | bytes 1048576
  67.6 0.4 collective-permute-done.10
  67.9 0.5 slice.57
  68.4 0.6 slice_reduce_fusion
  69.2 0.6 maximum_bitcast_fusion
  (77 shorter events, 2.5 us)
Async XLA Ops:
  0.6 7.0 %copy-start = (bf16[128,128,3,3]{1,0,3,2:T(8,128)(2,1)S(1)}, bf16[128,128,3,3]{1,0,3,2:T(8,128)(2,1)}, u32[]{:S(2)}) copy-start(bf16[128,128,3,3]{1,0,3,2:T(8,128)(2,1)} %param.24) | copy-start | bytes 884740
  1.8 6.1 %copy-start.3 = (bf16[64,3,3,3]{0,3,2,1:T(4,128)(2,1)S(1)}, bf16[64,3,3,3]{0,3,2,1:T(4,128)(2,1)}, u32[]{:S(2)}) copy-start(bf16[64,3,3,3]{0,3,2,1:T(4,128)(2,1)} %param.18) | copy-start | bytes 10372
  3.6 4.9 %copy-start.1 = (bf16[64,64,3,3]{1,0,3,2:T(8,128)(2,1)S(1)}, bf16[64,64,3,3]{1,0,3,2:T(8,128)(2,1)}, u32[]{:S(2)}) copy-start(bf16[64,64,3,3]{1,0,3,2:T(8,128)(2,1)} %param.20) | copy-start | bytes 221188
  3.6 6.5 %collective-permute-start = (f32[7,8,256]{2,1,0:T(8,128)S(1)}, f32[7,8,256]{2,1,0:T(8,128)S(1)}, u32[]{:S(2)}, u32[]{:S(2)}) collective-permute-start(f32[7,8,256]{2,1,0:T(8,128)S(1)} %get-tuple-element.21), channel_id=1, source_target_pairs={{0,1},{1,2},{2,3},{4,5},{5,6},{6,7},{8,9},{9,10},{10,11},{12,13},{... | collective-permute-start | bytes 172040 | tf_op jit(solution)/shard_map/ppermute | solution.py:391
  6.2 5.3 %collective-permute-start.1 = (f32[7,8,256]{2,1,0:T(8,128)S(1)}, f32[7,8,256]{2,1,0:T(8,128)S(1)}, u32[]{:S(2)}, u32[]{:S(2)}) collective-permute-start(f32[7,8,256]{2,1,0:T(8,128)S(1)} %get-tuple-element.23), channel_id=1, source_target_pairs={{1,0},{2,1},{3,2},{5,4},{6,5},{7,6},{9,8},{10,9},{11,10},{13,12},{... | collective-permute-start | bytes 172040 | tf_op jit(solution)/shard_map/ppermute | solution.py:391
  7.9 1.0 %copy-start.2 = (bf16[128,64,3,3]{0,1,3,2:T(8,128)(2,1)S(1)}, bf16[128,64,3,3]{0,1,3,2:T(8,128)(2,1)}, u32[]{:S(2)}) copy-start(bf16[128,64,3,3]{0,1,3,2:T(8,128)(2,1)} %param.22) | copy-start | bytes 442372
  7.9 1.1 %copy-start.5 = (f32[128]{0:T(128)S(1)}, f32[128]{0:T(128)}, u32[]{:S(2)}) copy-start(f32[128]{0:T(128)} %param.23) | copy-start | bytes 1540
  7.9 1.2 %copy-start.6 = (f32[128]{0:T(128)S(1)}, f32[128]{0:T(128)}, u32[]{:S(2)}) copy-start(f32[128]{0:T(128)} %param.25) | copy-start | bytes 1540
  7.9 1.3 %copy-start.7 = (f32[128]{0:T(128)S(1)}, f32[128]{0:T(128)}, u32[]{:S(2)}) copy-start(f32[128]{0:T(128)} %param.27) | copy-start | bytes 1540
  7.9 1.4 %copy-start.8 = (f32[64]{0:T(128)S(1)}, f32[64]{0:T(128)}, u32[]{:S(2)}) copy-start(f32[64]{0:T(128)} %param.19) | copy-start | bytes 772
  8.0 1.5 %copy-start.9 = (f32[64]{0:T(128)S(1)}, f32[64]{0:T(128)}, u32[]{:S(2)}) copy-start(f32[64]{0:T(128)} %param.21) | copy-start | bytes 772
  8.0 1.6 %copy-start.11 = (f32[3]{0:T(128)S(1)}, f32[3]{0:T(128)}, u32[]{:S(2)}) copy-start(f32[3]{0:T(128)} %param.16) | copy-start | bytes 40
  8.0 1.7 %copy-start.10 = (f32[64]{0:T(128)S(1)}, f32[64]{0:T(128)}, u32[]{:S(2)}) copy-start(f32[64]{0:T(128)} %param.26) | copy-start | bytes 772
  26.5 8.2 %collective-permute-start.2 = (bf16[2,128,128]{2,1,0:T(8,128)(2,1)S(1)}, bf16[2,128,128]{2,1,0:T(8,128)(2,1)S(1)}, u32[]{:S(2)}, u32[]{:S(2)}) collective-permute-start(bf16[2,128,128]{2,1,0:T(8,128)(2,1)S(1)} %get-tuple-element.49), channel_id=1, source_target_pairs={{0,1},{1,2},{2,3},{4,5},{5,6},{6,7},{8,9},{9,10},{10,11},{12,13},{... | collective-permute-start | bytes 196616 | tf_op jit(solution)/shard_map/ppermute | solution.py:391
  31.3 3.5 %collective-permute-start.3 = (bf16[2,128,128]{2,1,0:T(8,128)(2,1)S(1)}, bf16[2,128,128]{2,1,0:T(8,128)(2,1)S(1)}, u32[]{:S(2)}, u32[]{:S(2)}) collective-permute-start(bf16[2,128,128]{2,1,0:T(8,128)(2,1)S(1)} %get-tuple-element.48), channel_id=1, source_target_pairs={{1,0},{2,1},{3,2},{5,4},{6,5},{7,6},{9,8},{10,9},{11,10},{13,12},{... | collective-permute-start | bytes 196616 | tf_op jit(solution)/shard_map/ppermute | solution.py:391
  37.3 8.3 %collective-permute-start.4 = (bf16[3,64,256]{2,1,0:T(8,128)(2,1)S(1)}, bf16[3,64,256]{2,1,0:T(8,128)(2,1)S(1)}, u32[]{:S(2)}, u32[]{:S(2)}) collective-permute-start(bf16[3,64,256]{2,1,0:T(8,128)(2,1)S(1)} %get-tuple-element.47), channel_id=1, source_target_pairs={{0,1},{1,2},{2,3},{4,5},{5,6},{6,7},{8,9},{9,10},{10,11},{12,13},{... | collective-permute-start | bytes 294920 | tf_op jit(solution)/shard_map/ppermute | solution.py:391
  42.1 3.4 %collective-permute-start.5 = (bf16[3,64,256]{2,1,0:T(8,128)(2,1)S(1)}, bf16[3,64,256]{2,1,0:T(8,128)(2,1)S(1)}, u32[]{:S(2)}, u32[]{:S(2)}) collective-permute-start(bf16[3,64,256]{2,1,0:T(8,128)(2,1)S(1)} %get-tuple-element.46), channel_id=1, source_target_pairs={{1,0},{2,1},{3,2},{5,4},{6,5},{7,6},{9,8},{10,9},{11,10},{13,12},{... | collective-permute-start | bytes 294920 | tf_op jit(solution)/shard_map/ppermute | solution.py:391
  45.5 11.5 %copy-start.4 = (bf16[3,128,3,3]{1,3,2,0:T(4,128)(2,1)S(1)}, bf16[3,128,3,3]{1,3,2,0:T(4,128)(2,1)}, u32[]{:S(2)}) copy-start(bf16[3,128,3,3]{1,3,2,0:T(4,128)(2,1)} %param.15) | copy-start | bytes 20740
  48.1 3.6 %collective-permute-start.6 = (f32[2,24,128]{2,1,0:T(8,128)S(1)}, f32[2,24,128]{2,1,0:T(8,128)S(1)}, u32[]{:S(2)}, u32[]{:S(2)}) collective-permute-start(f32[2,24,128]{2,1,0:T(8,128)S(1)} %get-tuple-element.36), channel_id=1, source_target_pairs={{0,1},{1,0},{2,3},{3,2},{4,5},{5,4},{6,7},{7,6},{8,9},{9,8},{10,11... | collective-permute-start | bytes 73736 | tf_op jit(solution)/shard_map/ppermute | solution.py:382
  51.7 3.8 %collective-permute-start.7 = (f32[2,24,128]{2,1,0:T(8,128)S(1)}, f32[2,24,128]{2,1,0:T(8,128)S(1)}, u32[]{:S(2)}, u32[]{:S(2)}) collective-permute-start(f32[2,24,128]{2,1,0:T(8,128)S(1)} %add.35), channel_id=1, source_target_pairs={{0,2},{1,3},{2,0},{3,1},{4,6},{5,7},{6,4},{7,5},{8,10},{9,11},{10,... | collective-permute-start | bytes 73736 | tf_op jit(solution)/shard_map/ppermute | solution.py:382
  55.5 3.8 %collective-permute-start.8 = (f32[2,24,128]{2,1,0:T(8,128)S(1)}, f32[2,24,128]{2,1,0:T(8,128)S(1)}, u32[]{:S(2)}, u32[]{:S(2)}) collective-permute-start(f32[2,24,128]{2,1,0:T(8,128)S(1)} %add.36), channel_id=1, source_target_pairs={{0,4},{4,0},{8,12},{12,8},{16,20},{20,16},{24,28},{28,24},{1,5},{5... | collective-permute-start | bytes 73736 | tf_op jit(solution)/shard_map/ppermute | solution.py:382
  59.4 3.8 %collective-permute-start.9 = (f32[2,24,128]{2,1,0:T(8,128)S(1)}, f32[2,24,128]{2,1,0:T(8,128)S(1)}, u32[]{:S(2)}, u32[]{:S(2)}) collective-permute-start(f32[2,24,128]{2,1,0:T(8,128)S(1)} %add.37), channel_id=1, source_target_pairs={{0,8},{4,12},{8,0},{12,4},{16,24},{20,28},{24,16},{28,20},{1,9},{5... | collective-permute-start | bytes 73736 | tf_op jit(solution)/shard_map/ppermute | solution.py:382
  63.2 4.7 %collective-permute-start.10 = (f32[2,24,128]{2,1,0:T(8,128)S(1)}, f32[2,24,128]{2,1,0:T(8,128)S(1)}, u32[]{:S(2)}, u32[]{:S(2)}) collective-permute-start(f32[2,24,128]{2,1,0:T(8,128)S(1)} %add.38), channel_id=1, source_target_pairs={{0,16},{4,20},{8,24},{12,28},{16,0},{20,4},{24,8},{28,12},{1,17},{... | collective-permute-start | bytes 73736 | tf_op jit(solution)/shard_map/ppermute | solution.py:382
